TPU v7x, 128 devices: a whole 4x4x4 slice. The times are simulated.
128 devices in a mesh: sky: 16 (over x, z), depth: 8 (over y, core).
Axes of the slice: x: 4, y: 4, z: 4, core: 2. Of those that a mesh axis runs over, the one named last changes fastest.
Arguments:
- positions: float32 [3, 2048, 128], P(None, ('sky', 'depth')), may hold values from 0 to 1
- cell_points: int32 [2048], P(('sky', 'depth')), may hold values from 1 to 128
- target_log: float32 [16], replicated, may hold values from 8 to 20
- export_count: int32 [128, 128], P(('sky', 'depth')), may hold values from 0 to 3, as said below
- export_cell: int32 [128, 128, 3], P(('sky', 'depth')), may hold values from 0 to 15
- import_pair: int32 [128, 128, 3], P(('sky', 'depth')), may hold values from 0 to 15
- import_shift: int32 [3, 128, 128, 3], P(None, ('sky', 'depth')), may hold values from -1 to 1, as said below
Outputs:
- travel: float32 [3, 2048, 128], P(None, ('sky', 'depth'))
Inputs may be any that keep to these rules, and one draw needn't show every extreme that they name: export_count[s, t] counts the slots of export_cell[s, t] that are used; it is zero unless s and t are distinct devices whose sky indices differ by at most one modulo the sky axis's size and whose depth indices differ by at most one; in every draw some device t receives 3 cells from each such neighbour. For neighbouring devices t and s, components 0 and 2 of import_shift[:, t, s, k] are the sky step and the depth step from t's region to s's region (sky taken around the cycle), component 1 varies; all components are zero for devices that are not neighbours.
All inputs are finite; a program needn't handle non-finite values.
Results may differ from a plain program's by a relative error of at most 0.00022.
Values sent between devices are 32-bit elements; how exact they have to be, the bound alone decides.
No kernel may reach another device: no remote copies, remote signals or barrier semaphores. Data moves between devices by JAX's collectives and lax.ppermute only.
A program may use at most 64 MiB of HBM per device.

v0:
```python
import jax
import jax.numpy as jnp
from jax import lax
from jax.sharding import PartitionSpec as P

STEPS = 2
EPS_SQ = 0.0001
INV_WIDTH = 16.0
STEP_SIZE = 0.01
ROW_BLOCK = 8


def from_behind(array, axis, by):
    size = lax.axis_size(axis)
    return lax.ppermute(array, axis, [(i, (i + by) % size) for i in range(size)])


def from_behind_2(value, axis, steps):
    count = lax.axis_size(axis)
    initial, last = (max(0, -steps), min(count, count - steps))
    return lax.ppermute(value, axis, [(source, source + steps) for source in range(initial, last)])


def pair_geometry(left_pos, left_mask, right_pos, right_mask, shifts, centres):
    offsets = left_pos[:, :, :, None] - right_pos[:, :, None, :] - shifts[:, :, None, None]
    radius = jnp.sqrt(jnp.sum(offsets * offsets, axis=0) + EPS_SQ)
    weight = left_mask[:, :, None] * right_mask[:, None, :]
    scaled = (radius[None] - centres[:, None, None, None]) * INV_WIDTH
    kernel = jnp.exp(-0.5 * scaled * scaled)
    return (offsets, radius, weight, scaled, kernel)


def block_counts(left_pos, left_mask, right_pos, right_mask, shifts, centres):
    offsets, radius, weight, scaled, kernel = pair_geometry(
        left_pos, left_mask, right_pos, right_mask, shifts, centres
    )
    return jnp.sum(weight[None] * kernel, axis=(1, 2, 3))


def block_forces(left_pos, left_mask, right_pos, right_mask, shifts, centres, bin_pull):
    offsets, radius, weight, scaled, kernel = pair_geometry(
        left_pos, left_mask, right_pos, right_mask, shifts, centres
    )
    slopes = jnp.sum(bin_pull[:, None, None, None] * scaled * kernel, axis=0) * -INV_WIDTH
    strength = weight * slopes / radius
    pulled = strength[None] * offsets
    return (jnp.sum(pulled, axis=3), -jnp.sum(pulled, axis=2))


def take_block(left_pos, left_mask, right_pos, right_mask, shifts, first_row):
    return (
        lax.dynamic_slice_in_dim(left_pos, first_row, ROW_BLOCK, 1),
        lax.dynamic_slice_in_dim(left_mask, first_row, ROW_BLOCK, 0),
        lax.dynamic_slice_in_dim(right_pos, first_row, ROW_BLOCK, 1),
        lax.dynamic_slice_in_dim(right_mask, first_row, ROW_BLOCK, 0),
        lax.dynamic_slice_in_dim(shifts, first_row, ROW_BLOCK, 1),
    )


def ghost_counts(left_pos, left_mask, right_pos, right_mask, shifts, centres):
    block_total = left_pos.shape[1] // ROW_BLOCK

    def add_block(block_id, running):
        pieces = take_block(
            left_pos, left_mask, right_pos, right_mask, shifts, block_id * ROW_BLOCK
        )
        return running + block_counts(
            pieces[0], pieces[1], pieces[2], pieces[3], pieces[4], centres
        )

    return lax.fori_loop(0, block_total, add_block, jnp.zeros(centres.shape, jnp.float32))


def ghost_forces(left_pos, left_mask, right_pos, right_mask, shifts, centres, bin_pull):
    block_total = left_pos.shape[1] // ROW_BLOCK

    def add_block(block_id, buffers):
        first_row = block_id * ROW_BLOCK
        pieces = take_block(left_pos, left_mask, right_pos, right_mask, shifts, first_row)
        force_left, force_right = block_forces(
            pieces[0], pieces[1], pieces[2], pieces[3], pieces[4], centres, bin_pull
        )
        return (
            lax.dynamic_update_slice_in_dim(buffers[0], force_left, first_row, 1),
            lax.dynamic_update_slice_in_dim(buffers[1], force_right, first_row, 1),
        )

    empty = jnp.zeros(left_pos.shape, jnp.float32)
    return lax.fori_loop(0, block_total, add_block, (empty, empty))


def region_offsets():
    return [
        (across, along)
        for across in (-1, 0, 1)
        for along in (-1, 0, 1)
        if (across, along) != (0, 0)
    ]


def neighbour_table():
    sky_here = lax.axis_index("sky")
    depth_here = lax.axis_index("depth")
    sky_count = lax.axis_size("sky")
    depth_count = lax.axis_size("depth")
    near_ids = []
    near_valid = []
    for across, along in region_offsets():
        depth_there = depth_here + along
        inside = (depth_there >= 0) & (depth_there < depth_count)
        clamped = jnp.clip(depth_there, 0, depth_count - 1)
        near_ids.append((sky_here + across) % sky_count * depth_count + clamped)
        near_valid.append(inside)
    return (jnp.stack(near_ids), jnp.stack(near_valid))


def near_sizes(sizes_near):
    received = [None] * 8
    for index, (across, along) in enumerate(region_offsets()):
        piece = sizes_near[index]
        if across != 0:
            piece = from_behind(piece, "sky", across)
        if along != 0:
            piece = from_behind_2(piece, "depth", along)
        received[7 - index] = piece
    return jnp.stack(received)


def near_cells(cells_near):
    received = [None] * 8
    for index, (across, along) in enumerate(region_offsets()):
        piece = cells_near[:, index]
        if across != 0:
            piece = from_behind(piece, "sky", across)
        if along != 0:
            piece = from_behind_2(piece, "depth", along)
        received[7 - index] = piece
    return jnp.stack(received, axis=1)


def near_forces(forces_near):
    received = [None] * 8
    for index, (across, along) in enumerate(region_offsets()):
        piece = forces_near[:, index]
        if across != 0:
            piece = from_behind(piece, "sky", across)
        if along != 0:
            piece = from_behind_2(piece, "depth", along)
        received[7 - index] = piece
    return jnp.stack(received, axis=1)


def send_sizes(sizes_out, near_ids, near_valid):
    return near_sizes(sizes_out[near_ids] * near_valid[:, None].astype(jnp.int32))


def send_cells(coords, export_row, near_ids):
    peer_count, slot_count = export_row.shape
    outgoing = coords[:, export_row[near_ids].reshape(-1)].reshape(
        3, 8, slot_count, coords.shape[2]
    )
    return near_cells(outgoing)


def send_forces(forces_near):
    return near_forces(forces_near)


def body(positions, cell_points, target_log, export_count, export_cell, import_pair, import_shift):
    cell_count = positions.shape[1]
    points = positions.shape[2]
    slot_count = export_cell.shape[2]
    ghosts = 8 * slot_count
    centres = (jnp.arange(target_log.shape[0], dtype=jnp.float32) + 0.5) / INV_WIDTH
    point_ids = jnp.arange(points, dtype=jnp.int32)
    point_mask = (point_ids[None, :] < cell_points[:, None]).astype(jnp.float32)
    cell_ids = jnp.arange(cell_count, dtype=jnp.int32)
    near_ids, near_valid = neighbour_table()
    live_out = jnp.arange(slot_count, dtype=jnp.int32)[None, :] < export_count[0][:, None]
    sizes_out = jnp.where(live_out, cell_points[export_cell[0]], 0)
    sizes_in = send_sizes(sizes_out, near_ids, near_valid)
    ghost_mask = (point_ids[None, :] < sizes_in.reshape(-1)[:, None]).astype(jnp.float32)
    cells_near = export_cell[0][near_ids].reshape(-1)
    live_near = (live_out[near_ids] & near_valid[:, None]).reshape(-1)
    pair_cells = import_pair[0][near_ids].reshape(-1)
    shifts = import_shift[:, 0][:, near_ids].reshape(3, ghosts).astype(jnp.float32)
    left_mask = point_mask[pair_cells]
    onehot_pair = (pair_cells[:, None] == cell_ids[None, :]).astype(jnp.float32)
    onehot_out = ((cells_near[:, None] == cell_ids[None, :]) & live_near[:, None]).astype(
        jnp.float32
    )
    zero_shift = jnp.zeros((3, cell_count), jnp.float32)
    valid_local = jnp.sum(point_mask)
    coords = positions
    travel = jnp.zeros_like(positions)
    for iteration in range(STEPS):
        ghost_pos = send_cells(coords, export_cell[0], near_ids).reshape(3, ghosts, points)
        left_pos = coords[:, pair_cells]
        self_total = block_counts(coords, point_mask, coords, point_mask, zero_shift, centres)
        ghost_total = ghost_counts(left_pos, left_mask, ghost_pos, ghost_mask, shifts, centres)
        counts = lax.psum(0.5 * self_total + ghost_total, ("sky", "depth"))
        mean_count = jnp.mean(counts)
        bin_pull = (jnp.log(1.0 + counts) - target_log) * mean_count / (1.0 + counts)
        self_grad, unused_right = block_forces(
            coords, point_mask, coords, point_mask, zero_shift, centres, bin_pull
        )
        force_left, force_right = ghost_forces(
            left_pos, left_mask, ghost_pos, ghost_mask, shifts, centres, bin_pull
        )
        returned = send_forces(force_right.reshape(3, 8, slot_count, points)).reshape(
            3, ghosts, points
        )
        gradient = self_grad
        gradient = gradient + jnp.einsum(
            "gc,kgp->kcp", onehot_pair, force_left, precision=lax.Precision.HIGHEST
        )
        gradient = gradient + jnp.einsum(
            "gc,kgp->kcp", onehot_out, returned, precision=lax.Precision.HIGHEST
        )
        power_sum, valid_count = lax.psum(
            (jnp.sum(gradient * gradient), valid_local), ("sky", "depth")
        )
        grad_rms = jnp.sqrt(power_sum / (3.0 * valid_count) + 1e-06)
        move_dir = -gradient / grad_rms
        travel = travel + move_dir
        coords = coords + STEP_SIZE * move_dir
    return travel


def solution(mesh):
    in_specs = (
        P(None, ("sky", "depth"), None),
        P(("sky", "depth")),
        P(),
        P(("sky", "depth"), None),
        P(("sky", "depth"), None, None),
        P(("sky", "depth"), None, None),
        P(None, ("sky", "depth"), None, None),
    )
    out_specs = P(None, ("sky", "depth"), None)
    return jax.shard_map(body, mesh=mesh, in_specs=in_specs, out_specs=out_specs, check_vma=False)
```

profile of v0, /device:TPU:1, one launch (start us, length us, event | category | flops | bytes accessed | tf_op | source)
XLA Modules:
  0.0 525.2 jit_solution(16160007866016866266)
XLA Ops:
  0.9 1.9 fusion.81
  3.0 10.6 %fusion.60 = s32[128,3]{1,0:T(8,128)S(1)} fusion(s32[1,128,3]{2,1,0:T(8,128)S(1)} %copy.87, s32[]{:T(128)} %bitcast.31, s32[]{:T(128)} %bitcast.32, s32[]{:T(128)} %bitcast.33, s32[]{:T(128)} %bitcast.34, s32[]{:T(128)} %bitcast.35, s32[]{:T(128)} %bitcast.37, s32[]{:T(128)} %bitcast.36, s32[]{:T(128)} %bitcast.14, s32[]{:T(128)} %bitcast.16, s32[]{:T(128)} %bitcast.18, ...), kind=kLoop, calls=%fused_computation.175 | loop fusion | flops 13440 | bytes 3648 | tf_op jit(solution)/shard_map/jit(_where)/select_n | solution.py:180
  14.3 2.5 collective-permute-start
  19.7 4.6 collective-permute-start.5
  31.1 5.1 fusion.36
  39.6 4.8 collective-permute-start.7
  47.4 5.0 collective-permute-start.17
  55.5 2.1 collective-permute-start.4
  57.6 2.9 collective-permute-done.4
  60.4 2.0 collective-permute-start.8
  63.4 2.1 collective-permute-start.11
  65.6 2.9 collective-permute-done.11
  70.5 3.6 collective-permute-start.13
  74.9 3.4 collective-permute-start.19
  81.1 3.0 collective-permute-start.21
  84.2 5.6 %collective-permute-start.20 = (f32[3,3,128]{2,1,0:T(4,128)S(1)}, f32[3,3,128]{2,1,0:T(4,128)S(1)}, u32[]{:S(2)}, u32[]{:S(2)}) collective-permute-start(f32[3,3,128]{2,1,0:T(4,128)S(1)} %collective-permute-done.19), channel_id=1, source_target_pairs={{0,1},{1,2},{2,3},{3,4},{4,5},{5,6},{6,7},{8,9},{9,10},{10,11},{11... | collective-permute-start | bytes 13832 | tf_op jit(solution)/shard_map/ppermute | solution.py:21
  91.8 2.9 collective-permute-done.23
  94.8 10.7 %while.70 = (s32[]{:T(128)}, f32[16]{0:T(128)S(1)}, f32[24,128]{1,0:T(8,128)S(1)}, f32[24,128]{1,0:T(8,128)S(1)}, f32[3,24,128]{2,1,0:T(8,128)S(1)}, /*index=5*/...) while((s32[]{:T(128)}, f32[16]{0:T(128)S(1)}, ...), condition=%wide.region_5.6_spmd.clone, body=%wide.region_2.5_spmd.clone.sunk | while | flops 14286903 | bytes 3244889 | solution.py:71
  95.8 2.5 fusion.98
  99.3 2.5 fusion.98
  102.9 2.5 fusion.98
  105.6 62.9 %psum.38 = f32[16]{0:T(128)S(1)} all-reduce(f32[16]{0:T(128)S(1)} %multiply_add_fusion.2), channel_id=1, replica_groups=mesh['sky'=16,'depth'=8] {'sky','depth'}, use_global_device_ids=true, to_apply=%region_6.7 | all-reduce | flops 16 | bytes 128 | tf_op jit(solution)/shard_map/psum | solution.py:201
  169.6 5.4 %fusion.37 = f32[16,128,128]{2,1,0:T(8,128)S(1)} fusion(f32[16]{0:T(128)S(1)} %get-tuple-element.1089, f32[16]{0:T(128)S(1)} %add_multiply_fusion.4, f32[16,128,128]{2,1,0:T(8,128)S(1)} %get-tuple-element.1163), kind=kLoop, calls=%fused_computation.105 | loop fusion | flops 29097984 | bytes 2097280 | tf_op jit(solution)/shard_map/reduce_sum | solution.py:44
  175.4 14.3 %while.68 = (s32[]{:T(128)}, f32[3,24,128]{2,1,0:T(8,128)S(1)}, f32[3,24,128]{2,1,0:T(8,128)S(1)}, f32[24,128]{1,0:T(8,128)S(1)}, f32[24,128]{1,0:T(8,128)S(1)},...) while((s32[]{:T(128)}, f32[3,24,128]{2,1,0:T(8,128)S(1)}, ...), condition=%wide.region_15.16_spmd.clone, body=%wide.region_10.0_spmd.clone.sunk | while | flops 18740276 | bytes 4916107 | solution.py:89
  176.2 2.7 fusion.94
  180.9 2.7 fusion.94
  185.7 2.7 fusion.94
  194.3 3.1 collective-permute-start.29
  197.4 1.9 collective-permute-start.30
  199.4 3.6 collective-permute-start.25
  203.8 4.1 collective-permute-start.31
  210.2 3.7 collective-permute-start.33
  213.9 5.3 %collective-permute-start.32 = (f32[3,3,128]{2,1,0:T(4,128)S(1)}, f32[3,3,128]{2,1,0:T(4,128)S(1)}, u32[]{:S(2)}, u32[]{:S(2)}) collective-permute-start(f32[3,3,128]{2,1,0:T(4,128)S(1)} %collective-permute-done.31), channel_id=1, source_target_pairs={{0,1},{1,2},{2,3},{3,4},{4,5},{5,6},{6,7},{8,9},{9,10},{10,11},{11... | collective-permute-start | bytes 13832 | tf_op jit(solution)/shard_map/ppermute | solution.py:21
  219.3 1.9 collective-permute-start.35
  221.3 2.9 collective-permute-done.35
  225.0 62.3 %all-reduce = (f32[]{:T(128)}, f32[]{:T(128)}) all-reduce(f32[]{:T(128)} %get-tuple-element.1159, f32[]{:T(128)} %fusion.76), channel_id=1, replica_groups=mesh['sky'=16,'depth'=8] {'sky','depth'}, use_global_device_ids=true, to_apply=%region_17.18 | all-reduce | flops 2 | bytes 16 | tf_op jit(solution)/shard_map/psum | solution.py:220
  291.5 4.8 collective-permute-done.36
  296.3 4.4 collective-permute-start.37
  300.8 5.1 fusion.42
  306.6 1.9 collective-permute-start.41
  308.6 2.4 collective-permute-start.42
  311.0 4.8 collective-permute-start.43
  319.3 2.5 collective-permute-start.45
  321.8 4.7 collective-permute-start.44
  328.6 2.9 collective-permute-done.47
  331.5 10.7 %while.71 = (s32[]{:T(128)}, f32[16]{0:T(128)S(1)}, f32[24,128]{1,0:T(8,128)S(1)}, f32[24,128]{1,0:T(8,128)S(1)}, f32[3,24,128]{2,1,0:T(8,128)S(1)}, /*index=5*/...) while((s32[]{:T(128)}, f32[16]{0:T(128)S(1)}, ...), condition=%wide.region_25.26_spmd.clone, body=%wide.region_22.25_spmd.clone.sunk | while | flops 14286903 | bytes 3244889 | solution.py:71
  332.5 2.5 fusion.100
  336.1 2.5 fusion.100
  339.7 2.5 fusion.100
  342.2 62.2 %psum.41 = f32[16]{0:T(128)S(1)} all-reduce(f32[16]{0:T(128)S(1)} %multiply_add_fusion.1), channel_id=1, replica_groups=mesh['sky'=16,'depth'=8] {'sky','depth'}, use_global_device_ids=true, to_apply=%region_26.27 | all-reduce | flops 16 | bytes 128 | tf_op jit(solution)/shard_map/psum | solution.py:201
  405.7 5.4 %fusion.43 = f32[16,128,128]{2,1,0:T(8,128)S(1)} fusion(f32[16]{0:T(128)S(1)} %get-tuple-element.1087, f32[16,128,128]{2,1,0:T(8,128)S(1)} %add_sqrt_fusion.4, f32[16]{0:T(128)S(1)} %add_multiply_fusion.4), kind=kLoop, calls=%fused_computation.111 | loop fusion | flops 29097984 | bytes 2097280 | tf_op jit(solution)/shard_map/reduce_sum | solution.py:44
  411.5 14.3 %while.69 = (s32[]{:T(128)}, f32[3,24,128]{2,1,0:T(8,128)S(1)}, f32[3,24,128]{2,1,0:T(8,128)S(1)}, f32[24,128]{1,0:T(8,128)S(1)}, f32[24,128]{1,0:T(8,128)S(1)},...) while((s32[]{:T(128)}, f32[3,24,128]{2,1,0:T(8,128)S(1)}, ...), condition=%wide.region_35.36_spmd.clone, body=%wide.region_30.0_spmd.clone.sunk | while | flops 18740276 | bytes 4916107 | solution.py:89
  412.3 2.7 fusion.96
  417.0 2.7 fusion.96
  421.8 2.7 fusion.96
  428.7 2.0 collective-permute-start.51
  430.7 3.3 collective-permute-start.53
  434.0 1.9 collective-permute-start.54
  435.9 3.6 collective-permute-start.49
  440.3 3.8 collective-permute-start.55
  446.6 3.7 collective-permute-start.57
  450.2 5.3 %collective-permute-start.56 = (f32[3,3,128]{2,1,0:T(4,128)S(1)}, f32[3,3,128]{2,1,0:T(4,128)S(1)}, u32[]{:S(2)}, u32[]{:S(2)}) collective-permute-start(f32[3,3,128]{2,1,0:T(4,128)S(1)} %collective-permute-done.55), channel_id=1, source_target_pairs={{0,1},{1,2},{2,3},{3,4},{4,5},{5,6},{6,7},{8,9},{9,10},{10,11},{11... | collective-permute-start | bytes 13832 | tf_op jit(solution)/shard_map/ppermute | solution.py:21
  457.6 2.9 collective-permute-done.59
  461.3 62.2 %psum.42 = f32[]{:T(128)} all-reduce(f32[]{:T(128)} %get-tuple-element.1161), channel_id=1, replica_groups=mesh['sky'=16,'depth'=8] {'sky','depth'}, use_global_device_ids=true, to_apply=%region_37.38 | all-reduce | flops 1 | bytes 8 | tf_op jit(solution)/shard_map/psum | solution.py:220
  (337 shorter events, 76.0 us)
Async XLA Ops:
  0.0 26.5 %copy-start = (f32[3,16,128]{2,1,0:T(8,128)S(1)}, f32[3,16,128]{2,1,0:T(8,128)}, u32[]{:S(2)}) copy-start(f32[3,16,128]{2,1,0:T(8,128)} %param.15) | copy-start | bytes 73732
  0.0 27.6 %copy-start.3 = (s32[1,128]{1,0:T(1,128)S(1)}, s32[1,128]{1,0:T(1,128)}, u32[]{:S(2)}) copy-start(s32[1,128]{1,0:T(1,128)} %param.18) | copy-start | bytes 1540
  0.0 28.4 %copy-start.5 = (s32[1,128,3]{1,0,2:T(1,128)S(1)}, s32[1,128,3]{1,0,2:T(1,128)}, u32[]{:S(2)}) copy-start(s32[1,128,3]{1,0,2:T(1,128)} %param.20) | copy-start | bytes 4612
  14.3 23.4 %collective-permute-start = (s32[3]{0:T(128)S(1)}, s32[3]{0:T(128)S(1)}, u32[]{:S(2)}, u32[]{:S(2)}) collective-permute-start(s32[3]{0:T(128)S(1)} %get-tuple-element.1142), channel_id=1, source_target_pairs={{0,8},{8,16},{16,24},{24,32},{32,40},{40,48},{48,56},{56,64},{64,7... | collective-permute-start | bytes 44 | tf_op jit(solution)/shard_map/ppermute | solution.py:15
  16.7 22.9 %collective-permute-start.2 = (s32[3]{0:T(128)S(1)}, s32[3]{0:T(128)S(1)}, u32[]{:S(2)}, u32[]{:S(2)}) collective-permute-start(s32[3]{0:T(128)S(1)} %get-tuple-element.1141), channel_id=1, source_target_pairs={{0,8},{8,16},{16,24},{24,32},{32,40},{40,48},{48,56},{56,64},{64,7... | collective-permute-start | bytes 44 | tf_op jit(solution)/shard_map/ppermute | solution.py:15
  18.4 26.1 %collective-permute-start.3 = (s32[3]{0:T(128)S(1)}, s32[3]{0:T(128)S(1)}, u32[]{:S(2)}, u32[]{:S(2)}) collective-permute-start(s32[3]{0:T(128)S(1)} %get-tuple-element.1140), channel_id=1, source_target_pairs={{0,8},{8,16},{16,24},{24,32},{32,40},{40,48},{48,56},{56,64},{64,7... | collective-permute-start | bytes 44 | tf_op jit(solution)/shard_map/ppermute | solution.py:15
  19.7 24.9 %collective-permute-start.5 = (s32[3]{0:T(128)S(1)}, s32[3]{0:T(128)S(1)}, u32[]{:S(2)}, u32[]{:S(2)}) collective-permute-start(s32[3]{0:T(128)S(1)} %get-tuple-element.1139), channel_id=1, source_target_pairs={{0,1},{1,2},{2,3},{3,4},{4,5},{5,6},{6,7},{8,9},{9,10},{10,11},{11... | collective-permute-start | bytes 44 | tf_op jit(solution)/shard_map/ppermute | solution.py:21
  26.4 44.1 %collective-permute-start.12 = (f32[3,3,128]{2,1,0:T(4,128)S(1)}, f32[3,3,128]{2,1,0:T(4,128)S(1)}, u32[]{:S(2)}, u32[]{:S(2)}) collective-permute-start(f32[3,3,128]{2,1,0:T(4,128)S(1)} %get-tuple-element.1133), channel_id=1, source_target_pairs={{0,8},{8,16},{16,24},{24,32},{32,40},{40,48},{48,56},{56,64},{64,7... | collective-permute-start | bytes 13832 | tf_op jit(solution)/shard_map/ppermute | solution.py:15
  37.7 7.0 %collective-permute-start.6 = (s32[3]{0:T(128)S(1)}, s32[3]{0:T(128)S(1)}, u32[]{:S(2)}, u32[]{:S(2)}) collective-permute-start(s32[3]{0:T(128)S(1)} %get-tuple-element.1138), channel_id=1, source_target_pairs={{1,0},{2,1},{3,2},{4,3},{5,4},{6,5},{7,6},{9,8},{10,9},{11,10},{12... | collective-permute-start | bytes 44 | tf_op jit(solution)/shard_map/ppermute | solution.py:21
  39.6 6.4 %collective-permute-start.7 = (s32[3]{0:T(128)S(1)}, s32[3]{0:T(128)S(1)}, u32[]{:S(2)}, u32[]{:S(2)}) collective-permute-start(s32[3]{0:T(128)S(1)} %get-tuple-element.1137), channel_id=1, source_target_pairs={{0,120},{8,0},{16,8},{24,16},{32,24},{40,32},{48,40},{56,48},{64,5... | collective-permute-start | bytes 44 | tf_op jit(solution)/shard_map/ppermute | solution.py:15
  44.5 2.9 collective-permute-start.9
  44.6 7.9 %collective-permute-start.10 = (s32[3]{0:T(128)S(1)}, s32[3]{0:T(128)S(1)}, u32[]{:S(2)}, u32[]{:S(2)}) collective-permute-start(s32[3]{0:T(128)S(1)} %get-tuple-element.1135), channel_id=1, source_target_pairs={{0,120},{8,0},{16,8},{24,16},{32,24},{40,32},{48,40},{56,48},{64,5... | collective-permute-start | bytes 44 | tf_op jit(solution)/shard_map/ppermute | solution.py:15
  44.7 33.7 %collective-permute-start.14 = (f32[3,3,128]{2,1,0:T(4,128)S(1)}, f32[3,3,128]{2,1,0:T(4,128)S(1)}, u32[]{:S(2)}, u32[]{:S(2)}) collective-permute-start(f32[3,3,128]{2,1,0:T(4,128)S(1)} %get-tuple-element.1132), channel_id=1, source_target_pairs={{0,8},{8,16},{16,24},{24,32},{32,40},{40,48},{48,56},{56,64},{64,7... | collective-permute-start | bytes 13832 | tf_op jit(solution)/shard_map/ppermute | solution.py:15
  46.1 33.1 %collective-permute-start.15 = (f32[3,3,128]{2,1,0:T(4,128)S(1)}, f32[3,3,128]{2,1,0:T(4,128)S(1)}, u32[]{:S(2)}, u32[]{:S(2)}) collective-permute-start(f32[3,3,128]{2,1,0:T(4,128)S(1)} %get-tuple-element.1131), channel_id=1, source_target_pairs={{0,8},{8,16},{16,24},{24,32},{32,40},{40,48},{48,56},{56,64},{64,7... | collective-permute-start | bytes 13832 | tf_op jit(solution)/shard_map/ppermute | solution.py:15
  47.4 44.3 %collective-permute-start.17 = (f32[3,3,128]{2,1,0:T(4,128)S(1)}, f32[3,3,128]{2,1,0:T(4,128)S(1)}, u32[]{:S(2)}, u32[]{:S(2)}) collective-permute-start(f32[3,3,128]{2,1,0:T(4,128)S(1)} %get-tuple-element.1130), channel_id=1, source_target_pairs={{0,1},{1,2},{2,3},{3,4},{4,5},{5,6},{6,7},{8,9},{9,10},{10,11},{11... | collective-permute-start | bytes 13832 | tf_op jit(solution)/shard_map/ppermute | solution.py:21
  52.5 3.0 collective-permute-start.1
  55.5 5.0 collective-permute-start.4
  60.4 3.0 collective-permute-start.8
  63.4 5.0 collective-permute-start.11
  68.5 23.3 %collective-permute-start.18 = (f32[3,3,128]{2,1,0:T(4,128)S(1)}, f32[3,3,128]{2,1,0:T(4,128)S(1)}, u32[]{:S(2)}, u32[]{:S(2)}) collective-permute-start(f32[3,3,128]{2,1,0:T(4,128)S(1)} %get-tuple-element.1129), channel_id=1, source_target_pairs={{1,0},{2,1},{3,2},{4,3},{5,4},{6,5},{7,6},{9,8},{10,9},{11,10},{12... | collective-permute-start | bytes 13832 | tf_op jit(solution)/shard_map/ppermute | solution.py:21
  70.5 4.4 collective-permute-start.13
  74.9 6.2 %collective-permute-start.19 = (f32[3,3,128]{2,1,0:T(4,128)S(1)}, f32[3,3,128]{2,1,0:T(4,128)S(1)}, u32[]{:S(2)}, u32[]{:S(2)}) collective-permute-start(f32[3,3,128]{2,1,0:T(4,128)S(1)} %get-tuple-element.1128), channel_id=1, source_target_pairs={{0,120},{8,0},{16,8},{24,16},{32,24},{40,32},{48,40},{56,48},{64,5... | collective-permute-start | bytes 13832 | tf_op jit(solution)/shard_map/ppermute | solution.py:15
  78.4 5.8 %collective-permute-start.22 = (f32[3,3,128]{2,1,0:T(4,128)S(1)}, f32[3,3,128]{2,1,0:T(4,128)S(1)}, u32[]{:S(2)}, u32[]{:S(2)}) collective-permute-start(f32[3,3,128]{2,1,0:T(4,128)S(1)} %get-tuple-element.1127), channel_id=1, source_target_pairs={{0,120},{8,0},{16,8},{24,16},{32,24},{40,32},{48,40},{56,48},{64,5... | collective-permute-start | bytes 13832 | tf_op jit(solution)/shard_map/ppermute | solution.py:15
  79.2 10.6 %collective-permute-start.16 = (f32[3,3,128]{2,1,0:T(4,128)S(1)}, f32[3,3,128]{2,1,0:T(4,128)S(1)}, u32[]{:S(2)}, u32[]{:S(2)}) collective-permute-start(f32[3,3,128]{2,1,0:T(4,128)S(1)} %collective-permute-done.15), channel_id=1, source_target_pairs={{1,0},{2,1},{3,2},{4,3},{5,4},{6,5},{7,6},{9,8},{10,9},{11,10},{12... | collective-permute-start | bytes 13832 | tf_op jit(solution)/shard_map/ppermute | solution.py:21
  81.1 10.7 %collective-permute-start.21 = (f32[3,3,128]{2,1,0:T(4,128)S(1)}, f32[3,3,128]{2,1,0:T(4,128)S(1)}, u32[]{:S(2)}, u32[]{:S(2)}) collective-permute-start(f32[3,3,128]{2,1,0:T(4,128)S(1)} %get-tuple-element.1134), channel_id=1, source_target_pairs={{0,120},{8,0},{16,8},{24,16},{32,24},{40,32},{48,40},{56,48},{64,5... | collective-permute-start | bytes 13832 | tf_op jit(solution)/shard_map/ppermute | solution.py:15
  84.2 7.6 %collective-permute-start.20 = (f32[3,3,128]{2,1,0:T(4,128)S(1)}, f32[3,3,128]{2,1,0:T(4,128)S(1)}, u32[]{:S(2)}, u32[]{:S(2)}) collective-permute-start(f32[3,3,128]{2,1,0:T(4,128)S(1)} %collective-permute-done.19), channel_id=1, source_target_pairs={{0,1},{1,2},{2,3},{3,4},{4,5},{5,6},{6,7},{8,9},{9,10},{10,11},{11... | collective-permute-start | bytes 13832 | tf_op jit(solution)/shard_map/ppermute | solution.py:21
  89.8 4.9 collective-permute-start.23
  94.8 74.8 %copy-start.4 = (f32[16]{0:T(128)S(1)}, f32[16]{0:T(128)}, u32[]{:S(2)}) copy-start(f32[16]{0:T(128)} %param.17) | copy-start | bytes 196
  189.7 9.6 %collective-permute-start.24 = (f32[3,3,128]{2,1,0:T(4,128)S(1)}, f32[3,3,128]{2,1,0:T(4,128)S(1)}, u32[]{:S(2)}, u32[]{:S(2)}) collective-permute-start(f32[3,3,128]{2,1,0:T(4,128)S(1)} %get-tuple-element.1125), channel_id=1, source_target_pairs={{0,8},{8,16},{16,24},{24,32},{32,40},{40,48},{48,56},{56,64},{64,7... | collective-permute-start | bytes 13832 | tf_op jit(solution)/shard_map/ppermute | solution.py:15
  192.2 15.6 %collective-permute-start.26 = (f32[3,3,128]{2,1,0:T(4,128)S(1)}, f32[3,3,128]{2,1,0:T(4,128)S(1)}, u32[]{:S(2)}, u32[]{:S(2)}) collective-permute-start(f32[3,3,128]{2,1,0:T(4,128)S(1)} %get-tuple-element.1124), channel_id=1, source_target_pairs={{0,8},{8,16},{16,24},{24,32},{32,40},{40,48},{48,56},{56,64},{64,7... | collective-permute-start | bytes 13832 | tf_op jit(solution)/shard_map/ppermute | solution.py:15
  192.6 15.6 %collective-permute-start.27 = (f32[3,3,128]{2,1,0:T(4,128)S(1)}, f32[3,3,128]{2,1,0:T(4,128)S(1)}, u32[]{:S(2)}, u32[]{:S(2)}) collective-permute-start(f32[3,3,128]{2,1,0:T(4,128)S(1)} %get-tuple-element.1123), channel_id=1, source_target_pairs={{0,8},{8,16},{16,24},{24,32},{32,40},{40,48},{48,56},{56,64},{64,7... | collective-permute-start | bytes 13832 | tf_op jit(solution)/shard_map/ppermute | solution.py:15
  194.3 26.9 %collective-permute-start.29 = (f32[3,3,128]{2,1,0:T(4,128)S(1)}, f32[3,3,128]{2,1,0:T(4,128)S(1)}, u32[]{:S(2)}, u32[]{:S(2)}) collective-permute-start(f32[3,3,128]{2,1,0:T(4,128)S(1)} %get-tuple-element.1122), channel_id=1, source_target_pairs={{0,1},{1,2},{2,3},{3,4},{4,5},{5,6},{6,7},{8,9},{9,10},{10,11},{11... | collective-permute-start | bytes 13832 | tf_op jit(solution)/shard_map/ppermute | solution.py:21
  197.4 23.8 %collective-permute-start.30 = (f32[3,3,128]{2,1,0:T(4,128)S(1)}, f32[3,3,128]{2,1,0:T(4,128)S(1)}, u32[]{:S(2)}, u32[]{:S(2)}) collective-permute-start(f32[3,3,128]{2,1,0:T(4,128)S(1)} %get-tuple-element.1121), channel_id=1, source_target_pairs={{1,0},{2,1},{3,2},{4,3},{5,4},{6,5},{7,6},{9,8},{10,9},{11,10},{12... | collective-permute-start | bytes 13832 | tf_op jit(solution)/shard_map/ppermute | solution.py:21
  199.4 4.4 collective-permute-start.25
  203.8 6.4 %collective-permute-start.31 = (f32[3,3,128]{2,1,0:T(4,128)S(1)}, f32[3,3,128]{2,1,0:T(4,128)S(1)}, u32[]{:S(2)}, u32[]{:S(2)}) collective-permute-start(f32[3,3,128]{2,1,0:T(4,128)S(1)} %get-tuple-element.1120), channel_id=1, source_target_pairs={{0,120},{8,0},{16,8},{24,16},{32,24},{40,32},{48,40},{56,48},{64,5... | collective-permute-start | bytes 13832 | tf_op jit(solution)/shard_map/ppermute | solution.py:15
  207.8 6.1 %collective-permute-start.34 = (f32[3,3,128]{2,1,0:T(4,128)S(1)}, f32[3,3,128]{2,1,0:T(4,128)S(1)}, u32[]{:S(2)}, u32[]{:S(2)}) collective-permute-start(f32[3,3,128]{2,1,0:T(4,128)S(1)} %get-tuple-element.1119), channel_id=1, source_target_pairs={{0,120},{8,0},{16,8},{24,16},{32,24},{40,32},{48,40},{56,48},{64,5... | collective-permute-start | bytes 13832 | tf_op jit(solution)/shard_map/ppermute | solution.py:15
  208.2 11.0 %collective-permute-start.28 = (f32[3,3,128]{2,1,0:T(4,128)S(1)}, f32[3,3,128]{2,1,0:T(4,128)S(1)}, u32[]{:S(2)}, u32[]{:S(2)}) collective-permute-start(f32[3,3,128]{2,1,0:T(4,128)S(1)} %collective-permute-done.27), channel_id=1, source_target_pairs={{1,0},{2,1},{3,2},{4,3},{5,4},{6,5},{7,6},{9,8},{10,9},{11,10},{12... | collective-permute-start | bytes 13832 | tf_op jit(solution)/shard_map/ppermute | solution.py:21
  210.2 11.1 %collective-permute-start.33 = (f32[3,3,128]{2,1,0:T(4,128)S(1)}, f32[3,3,128]{2,1,0:T(4,128)S(1)}, u32[]{:S(2)}, u32[]{:S(2)}) collective-permute-start(f32[3,3,128]{2,1,0:T(4,128)S(1)} %get-tuple-element.1126), channel_id=1, source_target_pairs={{0,120},{8,0},{16,8},{24,16},{32,24},{40,32},{48,40},{56,48},{64,5... | collective-permute-start | bytes 13832 | tf_op jit(solution)/shard_map/ppermute | solution.py:15
  213.9 7.4 %collective-permute-start.32 = (f32[3,3,128]{2,1,0:T(4,128)S(1)}, f32[3,3,128]{2,1,0:T(4,128)S(1)}, u32[]{:S(2)}, u32[]{:S(2)}) collective-permute-start(f32[3,3,128]{2,1,0:T(4,128)S(1)} %collective-permute-done.31), channel_id=1, source_target_pairs={{0,1},{1,2},{2,3},{3,4},{4,5},{5,6},{6,7},{8,9},{9,10},{10,11},{11... | collective-permute-start | bytes 13832 | tf_op jit(solution)/shard_map/ppermute | solution.py:21
  219.3 4.9 collective-permute-start.35
  290.2 6.1 %collective-permute-start.36 = (f32[3,3,128]{2,1,0:T(4,128)S(1)}, f32[3,3,128]{2,1,0:T(4,128)S(1)}, u32[]{:S(2)}, u32[]{:S(2)}) collective-permute-start(f32[3,3,128]{2,1,0:T(4,128)S(1)} %bitcast.335), channel_id=1, source_target_pairs={{0,8},{8,16},{16,24},{24,32},{32,40},{40,48},{48,56},{56,64},{64,7... | collective-permute-start | bytes 13832 | tf_op jit(solution)/shard_map/ppermute | solution.py:15
  296.3 14.7 %collective-permute-start.37 = (f32[3,3,128]{2,1,0:T(4,128)S(1)}, f32[3,3,128]{2,1,0:T(4,128)S(1)}, u32[]{:S(2)}, u32[]{:S(2)}) collective-permute-start(f32[3,3,128]{2,1,0:T(4,128)S(1)} %collective-permute-done.36), channel_id=1, source_target_pairs={{0,1},{1,2},{2,3},{3,4},{4,5},{5,6},{6,7},{8,9},{9,10},{10,11},{11... | collective-permute-start | bytes 13832 | tf_op jit(solution)/shard_map/ppermute | solution.py:21
  306.5 9.4 %collective-permute-start.38 = (f32[3,3,128]{2,1,0:T(4,128)S(1)}, f32[3,3,128]{2,1,0:T(4,128)S(1)}, u32[]{:S(2)}, u32[]{:S(2)}) collective-permute-start(f32[3,3,128]{2,1,0:T(4,128)S(1)} %bitcast.332), channel_id=1, source_target_pairs={{0,8},{8,16},{16,24},{24,32},{32,40},{40,48},{48,56},{56,64},{64,7... | collective-permute-start | bytes 13832 | tf_op jit(solution)/shard_map/ppermute | solution.py:15
  306.6 10.8 %collective-permute-start.39 = (f32[3,3,128]{2,1,0:T(4,128)S(1)}, f32[3,3,128]{2,1,0:T(4,128)S(1)}, u32[]{:S(2)}, u32[]{:S(2)}) collective-permute-start(f32[3,3,128]{2,1,0:T(4,128)S(1)} %bitcast.331), channel_id=1, source_target_pairs={{0,8},{8,16},{16,24},{24,32},{32,40},{40,48},{48,56},{56,64},{64,7... | collective-permute-start | bytes 13832 | tf_op jit(solution)/shard_map/ppermute | solution.py:15
  306.6 21.8 %collective-permute-start.41 = (f32[3,3,128]{2,1,0:T(4,128)S(1)}, f32[3,3,128]{2,1,0:T(4,128)S(1)}, u32[]{:S(2)}, u32[]{:S(2)}) collective-permute-start(f32[3,3,128]{2,1,0:T(4,128)S(1)} %bitcast.330), channel_id=1, source_target_pairs={{0,1},{1,2},{2,3},{3,4},{4,5},{5,6},{6,7},{8,9},{9,10},{10,11},{11... | collective-permute-start | bytes 13832 | tf_op jit(solution)/shard_map/ppermute | solution.py:21
  308.6 19.9 %collective-permute-start.42 = (f32[3,3,128]{2,1,0:T(4,128)S(1)}, f32[3,3,128]{2,1,0:T(4,128)S(1)}, u32[]{:S(2)}, u32[]{:S(2)}) collective-permute-start(f32[3,3,128]{2,1,0:T(4,128)S(1)} %bitcast.329), channel_id=1, source_target_pairs={{1,0},{2,1},{3,2},{4,3},{5,4},{6,5},{7,6},{9,8},{10,9},{11,10},{12... | collective-permute-start | bytes 13832 | tf_op jit(solution)/shard_map/ppermute | solution.py:21
  311.0 8.2 %collective-permute-start.43 = (f32[3,3,128]{2,1,0:T(4,128)S(1)}, f32[3,3,128]{2,1,0:T(4,128)S(1)}, u32[]{:S(2)}, u32[]{:S(2)}) collective-permute-start(f32[3,3,128]{2,1,0:T(4,128)S(1)} %bitcast.334), channel_id=1, source_target_pairs={{0,120},{8,0},{16,8},{24,16},{32,24},{40,32},{48,40},{56,48},{64,5... | collective-permute-start | bytes 13832 | tf_op jit(solution)/shard_map/ppermute | solution.py:15
  315.9 5.9 %collective-permute-start.46 = (f32[3,3,128]{2,1,0:T(4,128)S(1)}, f32[3,3,128]{2,1,0:T(4,128)S(1)}, u32[]{:S(2)}, u32[]{:S(2)}) collective-permute-start(f32[3,3,128]{2,1,0:T(4,128)S(1)} %bitcast.333), channel_id=1, source_target_pairs={{0,120},{8,0},{16,8},{24,16},{32,24},{40,32},{48,40},{56,48},{64,5... | collective-permute-start | bytes 13832 | tf_op jit(solution)/shard_map/ppermute | solution.py:15
  317.3 9.2 %collective-permute-start.40 = (f32[3,3,128]{2,1,0:T(4,128)S(1)}, f32[3,3,128]{2,1,0:T(4,128)S(1)}, u32[]{:S(2)}, u32[]{:S(2)}) collective-permute-start(f32[3,3,128]{2,1,0:T(4,128)S(1)} %collective-permute-done.39), channel_id=1, source_target_pairs={{1,0},{2,1},{3,2},{4,3},{5,4},{6,5},{7,6},{9,8},{10,9},{11,10},{12... | collective-permute-start | bytes 13832 | tf_op jit(solution)/shard_map/ppermute | solution.py:21
  319.3 9.3 %collective-permute-start.45 = (f32[3,3,128]{2,1,0:T(4,128)S(1)}, f32[3,3,128]{2,1,0:T(4,128)S(1)}, u32[]{:S(2)}, u32[]{:S(2)}) collective-permute-start(f32[3,3,128]{2,1,0:T(4,128)S(1)} %bitcast.328), channel_id=1, source_target_pairs={{0,120},{8,0},{16,8},{24,16},{32,24},{40,32},{48,40},{56,48},{64,5... | collective-permute-start | bytes 13832 | tf_op jit(solution)/shard_map/ppermute | solution.py:15
  321.8 6.7 %collective-permute-start.44 = (f32[3,3,128]{2,1,0:T(4,128)S(1)}, f32[3,3,128]{2,1,0:T(4,128)S(1)}, u32[]{:S(2)}, u32[]{:S(2)}) collective-permute-start(f32[3,3,128]{2,1,0:T(4,128)S(1)} %collective-permute-done.43), channel_id=1, source_target_pairs={{0,1},{1,2},{2,3},{3,4},{4,5},{5,6},{6,7},{8,9},{9,10},{10,11},{11... | collective-permute-start | bytes 13832 | tf_op jit(solution)/shard_map/ppermute | solution.py:21
  326.5 4.9 collective-permute-start.47
  425.8 10.1 %collective-permute-start.48 = (f32[3,3,128]{2,1,0:T(4,128)S(1)}, f32[3,3,128]{2,1,0:T(4,128)S(1)}, u32[]{:S(2)}, u32[]{:S(2)}) collective-permute-start(f32[3,3,128]{2,1,0:T(4,128)S(1)} %get-tuple-element.1109), channel_id=1, source_target_pairs={{0,8},{8,16},{16,24},{24,32},{32,40},{40,48},{48,56},{56,64},{64,7... | collective-permute-start | bytes 13832 | tf_op jit(solution)/shard_map/ppermute | solution.py:15
  428.5 15.6 %collective-permute-start.50 = (f32[3,3,128]{2,1,0:T(4,128)S(1)}, f32[3,3,128]{2,1,0:T(4,128)S(1)}, u32[]{:S(2)}, u32[]{:S(2)}) collective-permute-start(f32[3,3,128]{2,1,0:T(4,128)S(1)} %get-tuple-element.1108), channel_id=1, source_target_pairs={{0,8},{8,16},{16,24},{24,32},{32,40},{40,48},{48,56},{56,64},{64,7... | collective-permute-start | bytes 13832 | tf_op jit(solution)/shard_map/ppermute | solution.py:15
  428.7 15.9 %collective-permute-start.51 = (f32[3,3,128]{2,1,0:T(4,128)S(1)}, f32[3,3,128]{2,1,0:T(4,128)S(1)}, u32[]{:S(2)}, u32[]{:S(2)}) collective-permute-start(f32[3,3,128]{2,1,0:T(4,128)S(1)} %get-tuple-element.1107), channel_id=1, source_target_pairs={{0,8},{8,16},{16,24},{24,32},{32,40},{40,48},{48,56},{56,64},{64,7... | collective-permute-start | bytes 13832 | tf_op jit(solution)/shard_map/ppermute | solution.py:15
  430.7 26.9 %collective-permute-start.53 = (f32[3,3,128]{2,1,0:T(4,128)S(1)}, f32[3,3,128]{2,1,0:T(4,128)S(1)}, u32[]{:S(2)}, u32[]{:S(2)}) collective-permute-start(f32[3,3,128]{2,1,0:T(4,128)S(1)} %get-tuple-element.1106), channel_id=1, source_target_pairs={{0,1},{1,2},{2,3},{3,4},{4,5},{5,6},{6,7},{8,9},{9,10},{10,11},{11... | collective-permute-start | bytes 13832 | tf_op jit(solution)/shard_map/ppermute | solution.py:21
  434.0 23.5 %collective-permute-start.54 = (f32[3,3,128]{2,1,0:T(4,128)S(1)}, f32[3,3,128]{2,1,0:T(4,128)S(1)}, u32[]{:S(2)}, u32[]{:S(2)}) collective-permute-start(f32[3,3,128]{2,1,0:T(4,128)S(1)} %get-tuple-element.1105), channel_id=1, source_target_pairs={{1,0},{2,1},{3,2},{4,3},{5,4},{6,5},{7,6},{9,8},{10,9},{11,10},{12... | collective-permute-start | bytes 13832 | tf_op jit(solution)/shard_map/ppermute | solution.py:21
  435.9 4.4 collective-permute-start.49
  440.3 6.2 %collective-permute-start.55 = (f32[3,3,128]{2,1,0:T(4,128)S(1)}, f32[3,3,128]{2,1,0:T(4,128)S(1)}, u32[]{:S(2)}, u32[]{:S(2)}) collective-permute-start(f32[3,3,128]{2,1,0:T(4,128)S(1)} %get-tuple-element.1104), channel_id=1, source_target_pairs={{0,120},{8,0},{16,8},{24,16},{32,24},{40,32},{48,40},{56,48},{64,5... | collective-permute-start | bytes 13832 | tf_op jit(solution)/shard_map/ppermute | solution.py:15
  444.1 6.1 %collective-permute-start.58 = (f32[3,3,128]{2,1,0:T(4,128)S(1)}, f32[3,3,128]{2,1,0:T(4,128)S(1)}, u32[]{:S(2)}, u32[]{:S(2)}) collective-permute-start(f32[3,3,128]{2,1,0:T(4,128)S(1)} %get-tuple-element.1103), channel_id=1, source_target_pairs={{0,120},{8,0},{16,8},{24,16},{32,24},{40,32},{48,40},{56,48},{64,5... | collective-permute-start | bytes 13832 | tf_op jit(solution)/shard_map/ppermute | solution.py:15
  444.6 10.9 %collective-permute-start.52 = (f32[3,3,128]{2,1,0:T(4,128)S(1)}, f32[3,3,128]{2,1,0:T(4,128)S(1)}, u32[]{:S(2)}, u32[]{:S(2)}) collective-permute-start(f32[3,3,128]{2,1,0:T(4,128)S(1)} %collective-permute-done.51), channel_id=1, source_target_pairs={{1,0},{2,1},{3,2},{4,3},{5,4},{6,5},{7,6},{9,8},{10,9},{11,10},{12... | collective-permute-start | bytes 13832 | tf_op jit(solution)/shard_map/ppermute | solution.py:21
  446.6 11.0 %collective-permute-start.57 = (f32[3,3,128]{2,1,0:T(4,128)S(1)}, f32[3,3,128]{2,1,0:T(4,128)S(1)}, u32[]{:S(2)}, u32[]{:S(2)}) collective-permute-start(f32[3,3,128]{2,1,0:T(4,128)S(1)} %get-tuple-element.1110), channel_id=1, source_target_pairs={{0,120},{8,0},{16,8},{24,16},{32,24},{40,32},{48,40},{56,48},{64,5... | collective-permute-start | bytes 13832 | tf_op jit(solution)/shard_map/ppermute | solution.py:15
  450.2 7.3 %collective-permute-start.56 = (f32[3,3,128]{2,1,0:T(4,128)S(1)}, f32[3,3,128]{2,1,0:T(4,128)S(1)}, u32[]{:S(2)}, u32[]{:S(2)}) collective-permute-start(f32[3,3,128]{2,1,0:T(4,128)S(1)} %collective-permute-done.55), channel_id=1, source_target_pairs={{0,1},{1,2},{2,3},{3,4},{4,5},{5,6},{6,7},{8,9},{9,10},{10,11},{11... | collective-permute-start | bytes 13832 | tf_op jit(solution)/shard_map/ppermute | solution.py:21
  455.6 4.9 collective-permute-start.59
  (2 other events, 52.8 us)
where the time goes:
time: 535 us; the launch traced here: 525 us
  blocking collectives  250 us (47%)
  starting transfers between devices  140 us (26%)
  other arithmetic  89.7 us (17%)
  waiting for transfers between devices  26.4 us (5%)
  local copies, waits for them, and re-layouts  12.1 us (2%)
    psum x2, blocking collectives, body(): counts = lax.psum(0.5 * self_total + ghost_total, ('sky', 'depth'))  125 us
    psum x2, blocking collectives, body(): lax.psum((jnp.sum(gradient * gradient), valid_local), ('sky', 'depth'))  124 us
    ppermute x30, starting transfers between devices, from_behind_2(): lax.ppermute(value, axis, [(source, source + steps) for source in range(i...  87.8 us
    ppermute x30, starting transfers between devices, from_behind(): lax.ppermute(array, axis, [(i, (i + by) % size) for i in range(size)])  52.4 us
    reduce_sum x8, other arithmetic, block_forces(): jnp.sum(bin_pull[:, None, None, None] * scaled * kernel, axis=0)  26.9 us
    reduce_sum x8, other arithmetic, block_counts(): return jnp.sum(weight[None] * kernel, axis=(1, 2, 3))  25.4 us
    ppermute x30, waiting for transfers between devices, from_behind_2(): lax.ppermute(value, axis, [(source, source + steps) for source in range(i...  21.5 us
  transfers between devices with their start and end apart: 60, of which 12 were waited for; matrix products, arithmetic and copies ran while one was open for 4% of the time, Pallas kernels for 0%

commit v1 on v0

--- a/solution.py
+++ b/solution.py
@@ -198,7 +198,7 @@
         left_pos = coords[:, pair_cells]
         self_total = block_counts(coords, point_mask, coords, point_mask, zero_shift, centres)
         ghost_total = ghost_counts(left_pos, left_mask, ghost_pos, ghost_mask, shifts, centres)
-        counts = lax.psum(0.5 * self_total + ghost_total, ("sky", "depth"))
+        counts = lax.psum(lax.psum(0.5 * self_total + ghost_total, "sky"), "depth")
         mean_count = jnp.mean(counts)
         bin_pull = (jnp.log(1.0 + counts) - target_log) * mean_count / (1.0 + counts)
         self_grad, unused_right = block_forces(

time: 535 us -> 500 us (0.935)
  blocking collectives: 250 us -> 221 us
    psum x2 -> x4, blocking collectives: 125 us -> 95.8 us  [body(): counts = lax.psum(lax.psum(0.5 * self_total + ghost_total, 'sky'), 'depth')]
  transfers between devices with their start and end apart: 60 -> 60, of which waited for: 12 -> 12; matrix products, arithmetic and copies ran while one was open for 4% -> 5% of each run, Pallas kernels for 0% -> 0%
where the time goes in v1:
time: 500 us; the launch traced here: 491 us
  blocking collectives  221 us (44%)
  starting transfers between devices  135 us (27%)
  other arithmetic  89.9 us (18%)
  waiting for transfers between devices  26.5 us (5%)
  local copies, waits for them, and re-layouts  12.1 us (2%)
    psum x2, blocking collectives, body(): lax.psum((jnp.sum(gradient * gradient), valid_local), ('sky', 'depth'))  125 us
    psum x4, blocking collectives, body(): counts = lax.psum(lax.psum(0.5 * self_total + ghost_total, 'sky'), 'depth')  95.8 us
    ppermute x30, starting transfers between devices, from_behind_2(): lax.ppermute(value, axis, [(source, source + steps) for source in range(i...  85.7 us
    ppermute x30, starting transfers between devices, from_behind(): lax.ppermute(array, axis, [(i, (i + by) % size) for i in range(size)])  48.9 us
    reduce_sum x8, other arithmetic, block_forces(): jnp.sum(bin_pull[:, None, None, None] * scaled * kernel, axis=0)  26.9 us
    reduce_sum x8, other arithmetic, block_counts(): return jnp.sum(weight[None] * kernel, axis=(1, 2, 3))  25.4 us
    ppermute x30, waiting for transfers between devices, from_behind_2(): lax.ppermute(value, axis, [(source, source + steps) for source in range(i...  21.5 us
    select_n x1, other arithmetic, body(): sizes_out = jnp.where(live_out, cell_points[export_cell[0]], 0)  10.7 us
  transfers between devices with their start and end apart: 60, of which 12 were waited for; matrix products, arithmetic and copies ran while one was open for 5% of the time, Pallas kernels for 0%

profile of v1, /device:TPU:1, one launch (start us, length us, event | category | flops | bytes accessed | tf_op | source)
XLA Modules:
  0.0 491.2 jit_solution(8858545971122071518)
XLA Ops:
  0.9 1.9 fusion.81
  3.0 10.7 %fusion.60 = s32[128,3]{1,0:T(8,128)S(1)} fusion(s32[1,128,3]{2,1,0:T(8,128)S(1)} %copy.87, s32[]{:T(128)} %bitcast.31, s32[]{:T(128)} %bitcast.32, s32[]{:T(128)} %bitcast.33, s32[]{:T(128)} %bitcast.34, s32[]{:T(128)} %bitcast.35, s32[]{:T(128)} %bitcast.37, s32[]{:T(128)} %bitcast.36, s32[]{:T(128)} %bitcast.14, s32[]{:T(128)} %bitcast.16, s32[]{:T(128)} %bitcast.18, ...), kind=kLoop, calls=%fused_computation.175 | loop fusion | flops 13440 | bytes 3648 | tf_op jit(solution)/shard_map/jit(_where)/select_n | solution.py:180
  14.3 2.5 collective-permute-start
  19.8 4.6 collective-permute-start.5
  31.3 5.1 %fusion.36 = f32[16]{0:T(128)S(1)} fusion(f32[16,128,128]{2,1,0:T(8,128)S(1)} %get-tuple-element.1164, f32[16]{0:T(128)S(1)} %add_multiply_fusion.4, f32[16,128,128]{2,1,0:T(8,128)S(1)} %get-tuple-element.1163), kind=kLoop, calls=%fused_computation.104 | loop fusion | flops 25165808 | bytes 2097280 | tf_op jit(solution)/shard_map/reduce_sum | solution.py:37
  37.8 1.9 collective-permute-start.6
  39.8 4.8 collective-permute-start.7
  47.5 5.0 %collective-permute-start.17 = (f32[3,3,128]{2,1,0:T(4,128)S(1)}, f32[3,3,128]{2,1,0:T(4,128)S(1)}, u32[]{:S(2)}, u32[]{:S(2)}) collective-permute-start(f32[3,3,128]{2,1,0:T(4,128)S(1)} %get-tuple-element.1130), channel_id=1, source_target_pairs={{0,1},{1,2},{2,3},{3,4},{4,5},{5,6},{6,7},{8,9},{9,10},{10,11},{11... | collective-permute-start | bytes 13832 | tf_op jit(solution)/shard_map/ppermute | solution.py:21
  52.6 1.9 collective-permute-start.1
  55.6 2.1 collective-permute-start.4
  57.7 2.9 collective-permute-done.4
  60.6 2.0 collective-permute-start.8
  63.6 2.1 collective-permute-start.11
  65.7 2.9 collective-permute-done.11
  70.6 3.6 collective-permute-start.13
  75.0 3.4 collective-permute-start.19
  81.3 3.0 collective-permute-start.21
  84.3 5.6 %collective-permute-start.20 = (f32[3,3,128]{2,1,0:T(4,128)S(1)}, f32[3,3,128]{2,1,0:T(4,128)S(1)}, u32[]{:S(2)}, u32[]{:S(2)}) collective-permute-start(f32[3,3,128]{2,1,0:T(4,128)S(1)} %collective-permute-done.19), channel_id=1, source_target_pairs={{0,1},{1,2},{2,3},{3,4},{4,5},{5,6},{6,7},{8,9},{9,10},{10,11},{11... | collective-permute-start | bytes 13832 | tf_op jit(solution)/shard_map/ppermute | solution.py:21
  92.0 2.9 collective-permute-done.23
  94.9 10.7 %while.70 = (s32[]{:T(128)}, f32[16]{0:T(128)S(1)}, f32[24,128]{1,0:T(8,128)S(1)}, f32[24,128]{1,0:T(8,128)S(1)}, f32[3,24,128]{2,1,0:T(8,128)S(1)}, /*index=5*/...) while((s32[]{:T(128)}, f32[16]{0:T(128)S(1)}, ...), condition=%wide.region_5.6_spmd.clone, body=%wide.region_2.5_spmd.clone.sunk | while | flops 14286903 | bytes 3244889 | solution.py:71
  95.9 2.5 fusion.98
  99.5 2.5 fusion.98
  103.0 2.5 fusion.98
  105.7 29.3 %psum.52 = f32[16]{0:T(128)S(1)} all-reduce(f32[16]{0:T(128)S(1)} %multiply_add_fusion.2), channel_id=1, replica_groups=mesh['sky'=16,'depth'=8] {'sky'}, use_global_device_ids=true, to_apply=%region_6.7 | all-reduce | flops 16 | bytes 128 | tf_op jit(solution)/shard_map/psum | solution.py:201
  135.0 18.5 %psum.53 = f32[16]{0:T(128)S(1)} all-reduce(f32[16]{0:T(128)S(1)} %psum.52), channel_id=1, replica_groups=mesh['sky'=16,'depth'=8] {'depth'}, use_global_device_ids=true, to_apply=%region_7.8 | all-reduce | flops 16 | bytes 128 | tf_op jit(solution)/shard_map/psum | solution.py:201
  154.8 5.4 %fusion.37 = f32[16,128,128]{2,1,0:T(8,128)S(1)} fusion(f32[16]{0:T(128)S(1)} %get-tuple-element.1089, f32[16]{0:T(128)S(1)} %add_multiply_fusion.4, f32[16,128,128]{2,1,0:T(8,128)S(1)} %get-tuple-element.1163), kind=kLoop, calls=%fused_computation.105 | loop fusion | flops 29097984 | bytes 2097280 | tf_op jit(solution)/shard_map/reduce_sum | solution.py:44
  160.6 14.3 %while.68 = (s32[]{:T(128)}, f32[3,24,128]{2,1,0:T(8,128)S(1)}, f32[3,24,128]{2,1,0:T(8,128)S(1)}, f32[24,128]{1,0:T(8,128)S(1)}, f32[24,128]{1,0:T(8,128)S(1)},...) while((s32[]{:T(128)}, f32[3,24,128]{2,1,0:T(8,128)S(1)}, ...), condition=%wide.region_16.17_spmd.clone, body=%wide.region_11.0_spmd.clone.sunk | while | flops 18740276 | bytes 4916107 | solution.py:89
  161.4 2.7 fusion.94
  166.1 2.7 fusion.94
  170.9 2.7 fusion.94
  179.6 2.4 collective-permute-start.30
  182.0 3.2 collective-permute-start.25
  185.9 4.7 collective-permute-start.31
  194.1 2.5 collective-permute-start.33
  196.6 5.6 %collective-permute-start.32 = (f32[3,3,128]{2,1,0:T(4,128)S(1)}, f32[3,3,128]{2,1,0:T(4,128)S(1)}, u32[]{:S(2)}, u32[]{:S(2)}) collective-permute-start(f32[3,3,128]{2,1,0:T(4,128)S(1)} %collective-permute-done.31), channel_id=1, source_target_pairs={{0,1},{1,2},{2,3},{3,4},{4,5},{5,6},{6,7},{8,9},{9,10},{10,11},{11... | collective-permute-start | bytes 13832 | tf_op jit(solution)/shard_map/ppermute | solution.py:21
  204.2 2.9 collective-permute-done.35
  207.9 62.5 %all-reduce = (f32[]{:T(128)}, f32[]{:T(128)}) all-reduce(f32[]{:T(128)} %get-tuple-element.1159, f32[]{:T(128)} %fusion.76), channel_id=1, replica_groups=mesh['sky'=16,'depth'=8] {'sky','depth'}, use_global_device_ids=true, to_apply=%region_18.19 | all-reduce | flops 2 | bytes 16 | tf_op jit(solution)/shard_map/psum | solution.py:220
  274.4 4.9 %collective-permute-done.36 = f32[3,3,128]{2,1,0:T(4,128)S(1)} collective-permute-done((f32[3,3,128]{2,1,0:T(4,128)S(1)}, f32[3,3,128]{2,1,0:T(4,128)S(1)}, u32[]{:S(2)}, u32[]{:S(2)}) %collective-permute-start.36) | collective-permute-done | bytes 4640 | tf_op jit(solution)/shard_map/ppermute | solution.py:15
  279.4 4.5 collective-permute-start.37
  283.9 5.1 %fusion.42 = f32[16]{0:T(128)S(1)} fusion(f32[16,128,128]{2,1,0:T(8,128)S(1)} %add_sqrt_fusion.4, f32[16,128,128]{2,1,0:T(8,128)S(1)} %get-tuple-element.1164, f32[16]{0:T(128)S(1)} %add_multiply_fusion.4), kind=kLoop, calls=%fused_computation.110 | loop fusion | flops 25165808 | bytes 2097280 | tf_op jit(solution)/shard_map/reduce_sum | solution.py:37
  289.8 1.9 collective-permute-start.41
  291.7 2.4 collective-permute-start.42
  294.2 4.8 collective-permute-start.43
  302.4 2.5 collective-permute-start.45
  304.9 4.7 collective-permute-start.44
  311.7 2.9 collective-permute-done.47
  314.7 10.7 %while.71 = (s32[]{:T(128)}, f32[16]{0:T(128)S(1)}, f32[24,128]{1,0:T(8,128)S(1)}, f32[24,128]{1,0:T(8,128)S(1)}, f32[3,24,128]{2,1,0:T(8,128)S(1)}, /*index=5*/...) while((s32[]{:T(128)}, f32[16]{0:T(128)S(1)}, ...), condition=%wide.region_26.27_spmd.clone, body=%wide.region_23.26_spmd.clone.sunk | while | flops 14286903 | bytes 3244889 | solution.py:71
  315.7 2.5 fusion.100
  319.2 2.5 fusion.100
  322.8 2.5 fusion.100
  325.3 30.2 %psum.56 = f32[16]{0:T(128)S(1)} all-reduce(f32[16]{0:T(128)S(1)} %multiply_add_fusion.1), channel_id=1, replica_groups=mesh['sky'=16,'depth'=8] {'sky'}, use_global_device_ids=true, to_apply=%region_27.28 | all-reduce | flops 16 | bytes 128 | tf_op jit(solution)/shard_map/psum | solution.py:201
  355.5 17.9 %psum.57 = f32[16]{0:T(128)S(1)} all-reduce(f32[16]{0:T(128)S(1)} %psum.56), channel_id=1, replica_groups=mesh['sky'=16,'depth'=8] {'depth'}, use_global_device_ids=true, to_apply=%region_28.29 | all-reduce | flops 16 | bytes 128 | tf_op jit(solution)/shard_map/psum | solution.py:201
  374.6 5.4 %fusion.43 = f32[16,128,128]{2,1,0:T(8,128)S(1)} fusion(f32[16]{0:T(128)S(1)} %get-tuple-element.1087, f32[16,128,128]{2,1,0:T(8,128)S(1)} %add_sqrt_fusion.4, f32[16]{0:T(128)S(1)} %add_multiply_fusion.4), kind=kLoop, calls=%fused_computation.111 | loop fusion | flops 29097984 | bytes 2097280 | tf_op jit(solution)/shard_map/reduce_sum | solution.py:44
  380.4 14.3 %while.69 = (s32[]{:T(128)}, f32[3,24,128]{2,1,0:T(8,128)S(1)}, f32[3,24,128]{2,1,0:T(8,128)S(1)}, f32[24,128]{1,0:T(8,128)S(1)}, f32[24,128]{1,0:T(8,128)S(1)},...) while((s32[]{:T(128)}, f32[3,24,128]{2,1,0:T(8,128)S(1)}, ...), condition=%wide.region_37.38_spmd.clone, body=%wide.region_32.0_spmd.clone.sunk | while | flops 18740276 | bytes 4916107 | solution.py:89
  381.2 2.7 fusion.96
  386.0 2.7 fusion.96
  390.7 2.7 fusion.96
  399.0 2.4 collective-permute-start.54
  401.5 3.2 collective-permute-start.49
  405.4 4.8 collective-permute-start.55
  413.5 2.5 collective-permute-start.57
  416.0 5.5 %collective-permute-start.56 = (f32[3,3,128]{2,1,0:T(4,128)S(1)}, f32[3,3,128]{2,1,0:T(4,128)S(1)}, u32[]{:S(2)}, u32[]{:S(2)}) collective-permute-start(f32[3,3,128]{2,1,0:T(4,128)S(1)} %collective-permute-done.55), channel_id=1, source_target_pairs={{0,1},{1,2},{2,3},{3,4},{4,5},{5,6},{6,7},{8,9},{9,10},{10,11},{11... | collective-permute-start | bytes 13832 | tf_op jit(solution)/shard_map/ppermute | solution.py:21
  423.6 2.9 collective-permute-done.59
  427.3 62.3 %psum.58 = f32[]{:T(128)} all-reduce(f32[]{:T(128)} %get-tuple-element.1161), channel_id=1, replica_groups=mesh['sky'=16,'depth'=8] {'sky','depth'}, use_global_device_ids=true, to_apply=%region_39.40 | all-reduce | flops 1 | bytes 8 | tf_op jit(solution)/shard_map/psum | solution.py:220
  (339 shorter events, 77.3 us)
Async XLA Ops:
  0.0 26.6 %copy-start = (f32[3,16,128]{2,1,0:T(8,128)S(1)}, f32[3,16,128]{2,1,0:T(8,128)}, u32[]{:S(2)}) copy-start(f32[3,16,128]{2,1,0:T(8,128)} %param.15) | copy-start | bytes 73732
  0.0 27.7 %copy-start.3 = (s32[1,128]{1,0:T(1,128)S(1)}, s32[1,128]{1,0:T(1,128)}, u32[]{:S(2)}) copy-start(s32[1,128]{1,0:T(1,128)} %param.18) | copy-start | bytes 1540
  0.0 28.5 %copy-start.5 = (s32[1,128,3]{1,0,2:T(1,128)S(1)}, s32[1,128,3]{1,0,2:T(1,128)}, u32[]{:S(2)}) copy-start(s32[1,128,3]{1,0,2:T(1,128)} %param.20) | copy-start | bytes 4612
  14.3 23.5 %collective-permute-start = (s32[3]{0:T(128)S(1)}, s32[3]{0:T(128)S(1)}, u32[]{:S(2)}, u32[]{:S(2)}) collective-permute-start(s32[3]{0:T(128)S(1)} %get-tuple-element.1142), channel_id=1, source_target_pairs={{0,8},{8,16},{16,24},{24,32},{32,40},{40,48},{48,56},{56,64},{64,7... | collective-permute-start | bytes 44 | tf_op jit(solution)/shard_map/ppermute | solution.py:15
  16.8 22.9 %collective-permute-start.2 = (s32[3]{0:T(128)S(1)}, s32[3]{0:T(128)S(1)}, u32[]{:S(2)}, u32[]{:S(2)}) collective-permute-start(s32[3]{0:T(128)S(1)} %get-tuple-element.1141), channel_id=1, source_target_pairs={{0,8},{8,16},{16,24},{24,32},{32,40},{40,48},{48,56},{56,64},{64,7... | collective-permute-start | bytes 44 | tf_op jit(solution)/shard_map/ppermute | solution.py:15
  18.5 26.1 %collective-permute-start.3 = (s32[3]{0:T(128)S(1)}, s32[3]{0:T(128)S(1)}, u32[]{:S(2)}, u32[]{:S(2)}) collective-permute-start(s32[3]{0:T(128)S(1)} %get-tuple-element.1140), channel_id=1, source_target_pairs={{0,8},{8,16},{16,24},{24,32},{32,40},{40,48},{48,56},{56,64},{64,7... | collective-permute-start | bytes 44 | tf_op jit(solution)/shard_map/ppermute | solution.py:15
  19.8 24.9 %collective-permute-start.5 = (s32[3]{0:T(128)S(1)}, s32[3]{0:T(128)S(1)}, u32[]{:S(2)}, u32[]{:S(2)}) collective-permute-start(s32[3]{0:T(128)S(1)} %get-tuple-element.1139), channel_id=1, source_target_pairs={{0,1},{1,2},{2,3},{3,4},{4,5},{5,6},{6,7},{8,9},{9,10},{10,11},{11... | collective-permute-start | bytes 44 | tf_op jit(solution)/shard_map/ppermute | solution.py:21
  26.5 44.2 %collective-permute-start.12 = (f32[3,3,128]{2,1,0:T(4,128)S(1)}, f32[3,3,128]{2,1,0:T(4,128)S(1)}, u32[]{:S(2)}, u32[]{:S(2)}) collective-permute-start(f32[3,3,128]{2,1,0:T(4,128)S(1)} %get-tuple-element.1133), channel_id=1, source_target_pairs={{0,8},{8,16},{16,24},{24,32},{32,40},{40,48},{48,56},{56,64},{64,7... | collective-permute-start | bytes 13832 | tf_op jit(solution)/shard_map/ppermute | solution.py:15
  37.8 7.0 %collective-permute-start.6 = (s32[3]{0:T(128)S(1)}, s32[3]{0:T(128)S(1)}, u32[]{:S(2)}, u32[]{:S(2)}) collective-permute-start(s32[3]{0:T(128)S(1)} %get-tuple-element.1138), channel_id=1, source_target_pairs={{1,0},{2,1},{3,2},{4,3},{5,4},{6,5},{7,6},{9,8},{10,9},{11,10},{12... | collective-permute-start | bytes 44 | tf_op jit(solution)/shard_map/ppermute | solution.py:21
  39.8 6.4 %collective-permute-start.7 = (s32[3]{0:T(128)S(1)}, s32[3]{0:T(128)S(1)}, u32[]{:S(2)}, u32[]{:S(2)}) collective-permute-start(s32[3]{0:T(128)S(1)} %get-tuple-element.1137), channel_id=1, source_target_pairs={{0,120},{8,0},{16,8},{24,16},{32,24},{40,32},{48,40},{56,48},{64,5... | collective-permute-start | bytes 44 | tf_op jit(solution)/shard_map/ppermute | solution.py:15
  44.6 2.9 collective-permute-start.9
  44.7 7.9 %collective-permute-start.10 = (s32[3]{0:T(128)S(1)}, s32[3]{0:T(128)S(1)}, u32[]{:S(2)}, u32[]{:S(2)}) collective-permute-start(s32[3]{0:T(128)S(1)} %get-tuple-element.1135), channel_id=1, source_target_pairs={{0,120},{8,0},{16,8},{24,16},{32,24},{40,32},{48,40},{56,48},{64,5... | collective-permute-start | bytes 44 | tf_op jit(solution)/shard_map/ppermute | solution.py:15
  44.8 33.7 %collective-permute-start.14 = (f32[3,3,128]{2,1,0:T(4,128)S(1)}, f32[3,3,128]{2,1,0:T(4,128)S(1)}, u32[]{:S(2)}, u32[]{:S(2)}) collective-permute-start(f32[3,3,128]{2,1,0:T(4,128)S(1)} %get-tuple-element.1132), channel_id=1, source_target_pairs={{0,8},{8,16},{16,24},{24,32},{32,40},{40,48},{48,56},{56,64},{64,7... | collective-permute-start | bytes 13832 | tf_op jit(solution)/shard_map/ppermute | solution.py:15
  46.2 33.1 %collective-permute-start.15 = (f32[3,3,128]{2,1,0:T(4,128)S(1)}, f32[3,3,128]{2,1,0:T(4,128)S(1)}, u32[]{:S(2)}, u32[]{:S(2)}) collective-permute-start(f32[3,3,128]{2,1,0:T(4,128)S(1)} %get-tuple-element.1131), channel_id=1, source_target_pairs={{0,8},{8,16},{16,24},{24,32},{32,40},{40,48},{48,56},{56,64},{64,7... | collective-permute-start | bytes 13832 | tf_op jit(solution)/shard_map/ppermute | solution.py:15
  47.5 44.3 %collective-permute-start.17 = (f32[3,3,128]{2,1,0:T(4,128)S(1)}, f32[3,3,128]{2,1,0:T(4,128)S(1)}, u32[]{:S(2)}, u32[]{:S(2)}) collective-permute-start(f32[3,3,128]{2,1,0:T(4,128)S(1)} %get-tuple-element.1130), channel_id=1, source_target_pairs={{0,1},{1,2},{2,3},{3,4},{4,5},{5,6},{6,7},{8,9},{9,10},{10,11},{11... | collective-permute-start | bytes 13832 | tf_op jit(solution)/shard_map/ppermute | solution.py:21
  52.6 3.0 collective-permute-start.1
  55.6 5.0 %collective-permute-start.4 = (s32[3]{0:T(128)S(1)}, s32[3]{0:T(128)S(1)}, u32[]{:S(2)}, u32[]{:S(2)}) collective-permute-start(s32[3]{0:T(128)S(1)} %collective-permute-done.3), channel_id=1, source_target_pairs={{1,0},{2,1},{3,2},{4,3},{5,4},{6,5},{7,6},{9,8},{10,9},{11,10},{12... | collective-permute-start | bytes 44 | tf_op jit(solution)/shard_map/ppermute | solution.py:21
  60.6 3.0 collective-permute-start.8
  63.6 5.0 %collective-permute-start.11 = (s32[3]{0:T(128)S(1)}, s32[3]{0:T(128)S(1)}, u32[]{:S(2)}, u32[]{:S(2)}) collective-permute-start(s32[3]{0:T(128)S(1)} %collective-permute-done.10), channel_id=1, source_target_pairs={{1,0},{2,1},{3,2},{4,3},{5,4},{6,5},{7,6},{9,8},{10,9},{11,10},{12... | collective-permute-start | bytes 44 | tf_op jit(solution)/shard_map/ppermute | solution.py:21
  68.6 23.3 %collective-permute-start.18 = (f32[3,3,128]{2,1,0:T(4,128)S(1)}, f32[3,3,128]{2,1,0:T(4,128)S(1)}, u32[]{:S(2)}, u32[]{:S(2)}) collective-permute-start(f32[3,3,128]{2,1,0:T(4,128)S(1)} %get-tuple-element.1129), channel_id=1, source_target_pairs={{1,0},{2,1},{3,2},{4,3},{5,4},{6,5},{7,6},{9,8},{10,9},{11,10},{12... | collective-permute-start | bytes 13832 | tf_op jit(solution)/shard_map/ppermute | solution.py:21
  70.6 4.4 collective-permute-start.13
  75.0 6.2 %collective-permute-start.19 = (f32[3,3,128]{2,1,0:T(4,128)S(1)}, f32[3,3,128]{2,1,0:T(4,128)S(1)}, u32[]{:S(2)}, u32[]{:S(2)}) collective-permute-start(f32[3,3,128]{2,1,0:T(4,128)S(1)} %get-tuple-element.1128), channel_id=1, source_target_pairs={{0,120},{8,0},{16,8},{24,16},{32,24},{40,32},{48,40},{56,48},{64,5... | collective-permute-start | bytes 13832 | tf_op jit(solution)/shard_map/ppermute | solution.py:15
  78.5 5.8 %collective-permute-start.22 = (f32[3,3,128]{2,1,0:T(4,128)S(1)}, f32[3,3,128]{2,1,0:T(4,128)S(1)}, u32[]{:S(2)}, u32[]{:S(2)}) collective-permute-start(f32[3,3,128]{2,1,0:T(4,128)S(1)} %get-tuple-element.1127), channel_id=1, source_target_pairs={{0,120},{8,0},{16,8},{24,16},{32,24},{40,32},{48,40},{56,48},{64,5... | collective-permute-start | bytes 13832 | tf_op jit(solution)/shard_map/ppermute | solution.py:15
  79.3 10.6 %collective-permute-start.16 = (f32[3,3,128]{2,1,0:T(4,128)S(1)}, f32[3,3,128]{2,1,0:T(4,128)S(1)}, u32[]{:S(2)}, u32[]{:S(2)}) collective-permute-start(f32[3,3,128]{2,1,0:T(4,128)S(1)} %collective-permute-done.15), channel_id=1, source_target_pairs={{1,0},{2,1},{3,2},{4,3},{5,4},{6,5},{7,6},{9,8},{10,9},{11,10},{12... | collective-permute-start | bytes 13832 | tf_op jit(solution)/shard_map/ppermute | solution.py:21
  81.3 10.7 %collective-permute-start.21 = (f32[3,3,128]{2,1,0:T(4,128)S(1)}, f32[3,3,128]{2,1,0:T(4,128)S(1)}, u32[]{:S(2)}, u32[]{:S(2)}) collective-permute-start(f32[3,3,128]{2,1,0:T(4,128)S(1)} %get-tuple-element.1134), channel_id=1, source_target_pairs={{0,120},{8,0},{16,8},{24,16},{32,24},{40,32},{48,40},{56,48},{64,5... | collective-permute-start | bytes 13832 | tf_op jit(solution)/shard_map/ppermute | solution.py:15
  84.3 7.6 %collective-permute-start.20 = (f32[3,3,128]{2,1,0:T(4,128)S(1)}, f32[3,3,128]{2,1,0:T(4,128)S(1)}, u32[]{:S(2)}, u32[]{:S(2)}) collective-permute-start(f32[3,3,128]{2,1,0:T(4,128)S(1)} %collective-permute-done.19), channel_id=1, source_target_pairs={{0,1},{1,2},{2,3},{3,4},{4,5},{5,6},{6,7},{8,9},{9,10},{10,11},{11... | collective-permute-start | bytes 13832 | tf_op jit(solution)/shard_map/ppermute | solution.py:21
  89.9 4.9 %collective-permute-start.23 = (f32[3,3,128]{2,1,0:T(4,128)S(1)}, f32[3,3,128]{2,1,0:T(4,128)S(1)}, u32[]{:S(2)}, u32[]{:S(2)}) collective-permute-start(f32[3,3,128]{2,1,0:T(4,128)S(1)} %collective-permute-done.22), channel_id=1, source_target_pairs={{1,0},{2,1},{3,2},{4,3},{5,4},{6,5},{7,6},{9,8},{10,9},{11,10},{12... | collective-permute-start | bytes 13832 | tf_op jit(solution)/shard_map/ppermute | solution.py:21
  94.9 59.8 %copy-start.4 = (f32[16]{0:T(128)S(1)}, f32[16]{0:T(128)}, u32[]{:S(2)}) copy-start(f32[16]{0:T(128)} %param.17) | copy-start | bytes 196
  174.9 7.1 %collective-permute-start.24 = (f32[3,3,128]{2,1,0:T(4,128)S(1)}, f32[3,3,128]{2,1,0:T(4,128)S(1)}, u32[]{:S(2)}, u32[]{:S(2)}) collective-permute-start(f32[3,3,128]{2,1,0:T(4,128)S(1)} %get-tuple-element.1125), channel_id=1, source_target_pairs={{0,8},{8,16},{16,24},{24,32},{32,40},{40,48},{48,56},{56,64},{64,7... | collective-permute-start | bytes 13832 | tf_op jit(solution)/shard_map/ppermute | solution.py:15
  177.5 13.2 %collective-permute-start.26 = (f32[3,3,128]{2,1,0:T(4,128)S(1)}, f32[3,3,128]{2,1,0:T(4,128)S(1)}, u32[]{:S(2)}, u32[]{:S(2)}) collective-permute-start(f32[3,3,128]{2,1,0:T(4,128)S(1)} %get-tuple-element.1124), channel_id=1, source_target_pairs={{0,8},{8,16},{16,24},{24,32},{32,40},{40,48},{48,56},{56,64},{64,7... | collective-permute-start | bytes 13832 | tf_op jit(solution)/shard_map/ppermute | solution.py:15
  177.6 14.6 %collective-permute-start.27 = (f32[3,3,128]{2,1,0:T(4,128)S(1)}, f32[3,3,128]{2,1,0:T(4,128)S(1)}, u32[]{:S(2)}, u32[]{:S(2)}) collective-permute-start(f32[3,3,128]{2,1,0:T(4,128)S(1)} %get-tuple-element.1123), channel_id=1, source_target_pairs={{0,8},{8,16},{16,24},{24,32},{32,40},{40,48},{48,56},{56,64},{64,7... | collective-permute-start | bytes 13832 | tf_op jit(solution)/shard_map/ppermute | solution.py:15
  177.7 26.4 %collective-permute-start.29 = (f32[3,3,128]{2,1,0:T(4,128)S(1)}, f32[3,3,128]{2,1,0:T(4,128)S(1)}, u32[]{:S(2)}, u32[]{:S(2)}) collective-permute-start(f32[3,3,128]{2,1,0:T(4,128)S(1)} %get-tuple-element.1122), channel_id=1, source_target_pairs={{0,1},{1,2},{2,3},{3,4},{4,5},{5,6},{6,7},{8,9},{9,10},{10,11},{11... | collective-permute-start | bytes 13832 | tf_op jit(solution)/shard_map/ppermute | solution.py:21
  179.6 24.5 %collective-permute-start.30 = (f32[3,3,128]{2,1,0:T(4,128)S(1)}, f32[3,3,128]{2,1,0:T(4,128)S(1)}, u32[]{:S(2)}, u32[]{:S(2)}) collective-permute-start(f32[3,3,128]{2,1,0:T(4,128)S(1)} %get-tuple-element.1121), channel_id=1, source_target_pairs={{1,0},{2,1},{3,2},{4,3},{5,4},{6,5},{7,6},{9,8},{10,9},{11,10},{12... | collective-permute-start | bytes 13832 | tf_op jit(solution)/shard_map/ppermute | solution.py:21
  182.0 3.9 collective-permute-start.25
  185.9 8.1 %collective-permute-start.31 = (f32[3,3,128]{2,1,0:T(4,128)S(1)}, f32[3,3,128]{2,1,0:T(4,128)S(1)}, u32[]{:S(2)}, u32[]{:S(2)}) collective-permute-start(f32[3,3,128]{2,1,0:T(4,128)S(1)} %get-tuple-element.1120), channel_id=1, source_target_pairs={{0,120},{8,0},{16,8},{24,16},{32,24},{40,32},{48,40},{56,48},{64,5... | collective-permute-start | bytes 13832 | tf_op jit(solution)/shard_map/ppermute | solution.py:15
  190.7 5.9 %collective-permute-start.34 = (f32[3,3,128]{2,1,0:T(4,128)S(1)}, f32[3,3,128]{2,1,0:T(4,128)S(1)}, u32[]{:S(2)}, u32[]{:S(2)}) collective-permute-start(f32[3,3,128]{2,1,0:T(4,128)S(1)} %get-tuple-element.1119), channel_id=1, source_target_pairs={{0,120},{8,0},{16,8},{24,16},{32,24},{40,32},{48,40},{56,48},{64,5... | collective-permute-start | bytes 13832 | tf_op jit(solution)/shard_map/ppermute | solution.py:15
  192.2 10.0 %collective-permute-start.28 = (f32[3,3,128]{2,1,0:T(4,128)S(1)}, f32[3,3,128]{2,1,0:T(4,128)S(1)}, u32[]{:S(2)}, u32[]{:S(2)}) collective-permute-start(f32[3,3,128]{2,1,0:T(4,128)S(1)} %collective-permute-done.27), channel_id=1, source_target_pairs={{1,0},{2,1},{3,2},{4,3},{5,4},{6,5},{7,6},{9,8},{10,9},{11,10},{12... | collective-permute-start | bytes 13832 | tf_op jit(solution)/shard_map/ppermute | solution.py:21
  194.1 10.1 %collective-permute-start.33 = (f32[3,3,128]{2,1,0:T(4,128)S(1)}, f32[3,3,128]{2,1,0:T(4,128)S(1)}, u32[]{:S(2)}, u32[]{:S(2)}) collective-permute-start(f32[3,3,128]{2,1,0:T(4,128)S(1)} %get-tuple-element.1126), channel_id=1, source_target_pairs={{0,120},{8,0},{16,8},{24,16},{32,24},{40,32},{48,40},{56,48},{64,5... | collective-permute-start | bytes 13832 | tf_op jit(solution)/shard_map/ppermute | solution.py:15
  196.6 7.6 %collective-permute-start.32 = (f32[3,3,128]{2,1,0:T(4,128)S(1)}, f32[3,3,128]{2,1,0:T(4,128)S(1)}, u32[]{:S(2)}, u32[]{:S(2)}) collective-permute-start(f32[3,3,128]{2,1,0:T(4,128)S(1)} %collective-permute-done.31), channel_id=1, source_target_pairs={{0,1},{1,2},{2,3},{3,4},{4,5},{5,6},{6,7},{8,9},{9,10},{10,11},{11... | collective-permute-start | bytes 13832 | tf_op jit(solution)/shard_map/ppermute | solution.py:21
  202.1 4.9 %collective-permute-start.35 = (f32[3,3,128]{2,1,0:T(4,128)S(1)}, f32[3,3,128]{2,1,0:T(4,128)S(1)}, u32[]{:S(2)}, u32[]{:S(2)}) collective-permute-start(f32[3,3,128]{2,1,0:T(4,128)S(1)} %collective-permute-done.34), channel_id=1, source_target_pairs={{1,0},{2,1},{3,2},{4,3},{5,4},{6,5},{7,6},{9,8},{10,9},{11,10},{12... | collective-permute-start | bytes 13832 | tf_op jit(solution)/shard_map/ppermute | solution.py:21
  273.5 5.9 %collective-permute-start.36 = (f32[3,3,128]{2,1,0:T(4,128)S(1)}, f32[3,3,128]{2,1,0:T(4,128)S(1)}, u32[]{:S(2)}, u32[]{:S(2)}) collective-permute-start(f32[3,3,128]{2,1,0:T(4,128)S(1)} %bitcast.335), channel_id=1, source_target_pairs={{0,8},{8,16},{16,24},{24,32},{32,40},{40,48},{48,56},{56,64},{64,7... | collective-permute-start | bytes 13832 | tf_op jit(solution)/shard_map/ppermute | solution.py:15
  279.4 14.8 %collective-permute-start.37 = (f32[3,3,128]{2,1,0:T(4,128)S(1)}, f32[3,3,128]{2,1,0:T(4,128)S(1)}, u32[]{:S(2)}, u32[]{:S(2)}) collective-permute-start(f32[3,3,128]{2,1,0:T(4,128)S(1)} %collective-permute-done.36), channel_id=1, source_target_pairs={{0,1},{1,2},{2,3},{3,4},{4,5},{5,6},{6,7},{8,9},{9,10},{10,11},{11... | collective-permute-start | bytes 13832 | tf_op jit(solution)/shard_map/ppermute | solution.py:21
  289.6 9.4 %collective-permute-start.38 = (f32[3,3,128]{2,1,0:T(4,128)S(1)}, f32[3,3,128]{2,1,0:T(4,128)S(1)}, u32[]{:S(2)}, u32[]{:S(2)}) collective-permute-start(f32[3,3,128]{2,1,0:T(4,128)S(1)} %bitcast.332), channel_id=1, source_target_pairs={{0,8},{8,16},{16,24},{24,32},{32,40},{40,48},{48,56},{56,64},{64,7... | collective-permute-start | bytes 13832 | tf_op jit(solution)/shard_map/ppermute | solution.py:15
  289.7 10.8 %collective-permute-start.39 = (f32[3,3,128]{2,1,0:T(4,128)S(1)}, f32[3,3,128]{2,1,0:T(4,128)S(1)}, u32[]{:S(2)}, u32[]{:S(2)}) collective-permute-start(f32[3,3,128]{2,1,0:T(4,128)S(1)} %bitcast.331), channel_id=1, source_target_pairs={{0,8},{8,16},{16,24},{24,32},{32,40},{40,48},{48,56},{56,64},{64,7... | collective-permute-start | bytes 13832 | tf_op jit(solution)/shard_map/ppermute | solution.py:15
  289.8 21.8 %collective-permute-start.41 = (f32[3,3,128]{2,1,0:T(4,128)S(1)}, f32[3,3,128]{2,1,0:T(4,128)S(1)}, u32[]{:S(2)}, u32[]{:S(2)}) collective-permute-start(f32[3,3,128]{2,1,0:T(4,128)S(1)} %bitcast.330), channel_id=1, source_target_pairs={{0,1},{1,2},{2,3},{3,4},{4,5},{5,6},{6,7},{8,9},{9,10},{10,11},{11... | collective-permute-start | bytes 13832 | tf_op jit(solution)/shard_map/ppermute | solution.py:21
  291.7 19.9 %collective-permute-start.42 = (f32[3,3,128]{2,1,0:T(4,128)S(1)}, f32[3,3,128]{2,1,0:T(4,128)S(1)}, u32[]{:S(2)}, u32[]{:S(2)}) collective-permute-start(f32[3,3,128]{2,1,0:T(4,128)S(1)} %bitcast.329), channel_id=1, source_target_pairs={{1,0},{2,1},{3,2},{4,3},{5,4},{6,5},{7,6},{9,8},{10,9},{11,10},{12... | collective-permute-start | bytes 13832 | tf_op jit(solution)/shard_map/ppermute | solution.py:21
  294.2 8.2 %collective-permute-start.43 = (f32[3,3,128]{2,1,0:T(4,128)S(1)}, f32[3,3,128]{2,1,0:T(4,128)S(1)}, u32[]{:S(2)}, u32[]{:S(2)}) collective-permute-start(f32[3,3,128]{2,1,0:T(4,128)S(1)} %bitcast.334), channel_id=1, source_target_pairs={{0,120},{8,0},{16,8},{24,16},{32,24},{40,32},{48,40},{56,48},{64,5... | collective-permute-start | bytes 13832 | tf_op jit(solution)/shard_map/ppermute | solution.py:15
  299.0 5.9 %collective-permute-start.46 = (f32[3,3,128]{2,1,0:T(4,128)S(1)}, f32[3,3,128]{2,1,0:T(4,128)S(1)}, u32[]{:S(2)}, u32[]{:S(2)}) collective-permute-start(f32[3,3,128]{2,1,0:T(4,128)S(1)} %bitcast.333), channel_id=1, source_target_pairs={{0,120},{8,0},{16,8},{24,16},{32,24},{40,32},{48,40},{56,48},{64,5... | collective-permute-start | bytes 13832 | tf_op jit(solution)/shard_map/ppermute | solution.py:15
  300.4 9.2 %collective-permute-start.40 = (f32[3,3,128]{2,1,0:T(4,128)S(1)}, f32[3,3,128]{2,1,0:T(4,128)S(1)}, u32[]{:S(2)}, u32[]{:S(2)}) collective-permute-start(f32[3,3,128]{2,1,0:T(4,128)S(1)} %collective-permute-done.39), channel_id=1, source_target_pairs={{1,0},{2,1},{3,2},{4,3},{5,4},{6,5},{7,6},{9,8},{10,9},{11,10},{12... | collective-permute-start | bytes 13832 | tf_op jit(solution)/shard_map/ppermute | solution.py:21
  302.4 9.3 %collective-permute-start.45 = (f32[3,3,128]{2,1,0:T(4,128)S(1)}, f32[3,3,128]{2,1,0:T(4,128)S(1)}, u32[]{:S(2)}, u32[]{:S(2)}) collective-permute-start(f32[3,3,128]{2,1,0:T(4,128)S(1)} %bitcast.328), channel_id=1, source_target_pairs={{0,120},{8,0},{16,8},{24,16},{32,24},{40,32},{48,40},{56,48},{64,5... | collective-permute-start | bytes 13832 | tf_op jit(solution)/shard_map/ppermute | solution.py:15
  304.9 6.7 %collective-permute-start.44 = (f32[3,3,128]{2,1,0:T(4,128)S(1)}, f32[3,3,128]{2,1,0:T(4,128)S(1)}, u32[]{:S(2)}, u32[]{:S(2)}) collective-permute-start(f32[3,3,128]{2,1,0:T(4,128)S(1)} %collective-permute-done.43), channel_id=1, source_target_pairs={{0,1},{1,2},{2,3},{3,4},{4,5},{5,6},{6,7},{8,9},{9,10},{10,11},{11... | collective-permute-start | bytes 13832 | tf_op jit(solution)/shard_map/ppermute | solution.py:21
  309.7 4.9 %collective-permute-start.47 = (f32[3,3,128]{2,1,0:T(4,128)S(1)}, f32[3,3,128]{2,1,0:T(4,128)S(1)}, u32[]{:S(2)}, u32[]{:S(2)}) collective-permute-start(f32[3,3,128]{2,1,0:T(4,128)S(1)} %collective-permute-done.46), channel_id=1, source_target_pairs={{1,0},{2,1},{3,2},{4,3},{5,4},{6,5},{7,6},{9,8},{10,9},{11,10},{12... | collective-permute-start | bytes 13832 | tf_op jit(solution)/shard_map/ppermute | solution.py:21
  394.7 6.7 %collective-permute-start.48 = (f32[3,3,128]{2,1,0:T(4,128)S(1)}, f32[3,3,128]{2,1,0:T(4,128)S(1)}, u32[]{:S(2)}, u32[]{:S(2)}) collective-permute-start(f32[3,3,128]{2,1,0:T(4,128)S(1)} %get-tuple-element.1109), channel_id=1, source_target_pairs={{0,8},{8,16},{16,24},{24,32},{32,40},{40,48},{48,56},{56,64},{64,7... | collective-permute-start | bytes 13832 | tf_op jit(solution)/shard_map/ppermute | solution.py:15
  396.9 13.2 %collective-permute-start.50 = (f32[3,3,128]{2,1,0:T(4,128)S(1)}, f32[3,3,128]{2,1,0:T(4,128)S(1)}, u32[]{:S(2)}, u32[]{:S(2)}) collective-permute-start(f32[3,3,128]{2,1,0:T(4,128)S(1)} %get-tuple-element.1108), channel_id=1, source_target_pairs={{0,8},{8,16},{16,24},{24,32},{32,40},{40,48},{48,56},{56,64},{64,7... | collective-permute-start | bytes 13832 | tf_op jit(solution)/shard_map/ppermute | solution.py:15
  397.0 14.6 %collective-permute-start.51 = (f32[3,3,128]{2,1,0:T(4,128)S(1)}, f32[3,3,128]{2,1,0:T(4,128)S(1)}, u32[]{:S(2)}, u32[]{:S(2)}) collective-permute-start(f32[3,3,128]{2,1,0:T(4,128)S(1)} %get-tuple-element.1107), channel_id=1, source_target_pairs={{0,8},{8,16},{16,24},{24,32},{32,40},{40,48},{48,56},{56,64},{64,7... | collective-permute-start | bytes 13832 | tf_op jit(solution)/shard_map/ppermute | solution.py:15
  397.1 26.4 %collective-permute-start.53 = (f32[3,3,128]{2,1,0:T(4,128)S(1)}, f32[3,3,128]{2,1,0:T(4,128)S(1)}, u32[]{:S(2)}, u32[]{:S(2)}) collective-permute-start(f32[3,3,128]{2,1,0:T(4,128)S(1)} %get-tuple-element.1106), channel_id=1, source_target_pairs={{0,1},{1,2},{2,3},{3,4},{4,5},{5,6},{6,7},{8,9},{9,10},{10,11},{11... | collective-permute-start | bytes 13832 | tf_op jit(solution)/shard_map/ppermute | solution.py:21
  399.0 24.5 %collective-permute-start.54 = (f32[3,3,128]{2,1,0:T(4,128)S(1)}, f32[3,3,128]{2,1,0:T(4,128)S(1)}, u32[]{:S(2)}, u32[]{:S(2)}) collective-permute-start(f32[3,3,128]{2,1,0:T(4,128)S(1)} %get-tuple-element.1105), channel_id=1, source_target_pairs={{1,0},{2,1},{3,2},{4,3},{5,4},{6,5},{7,6},{9,8},{10,9},{11,10},{12... | collective-permute-start | bytes 13832 | tf_op jit(solution)/shard_map/ppermute | solution.py:21
  401.5 3.9 collective-permute-start.49
  405.4 8.1 %collective-permute-start.55 = (f32[3,3,128]{2,1,0:T(4,128)S(1)}, f32[3,3,128]{2,1,0:T(4,128)S(1)}, u32[]{:S(2)}, u32[]{:S(2)}) collective-permute-start(f32[3,3,128]{2,1,0:T(4,128)S(1)} %get-tuple-element.1104), channel_id=1, source_target_pairs={{0,120},{8,0},{16,8},{24,16},{32,24},{40,32},{48,40},{56,48},{64,5... | collective-permute-start | bytes 13832 | tf_op jit(solution)/shard_map/ppermute | solution.py:15
  410.1 5.9 %collective-permute-start.58 = (f32[3,3,128]{2,1,0:T(4,128)S(1)}, f32[3,3,128]{2,1,0:T(4,128)S(1)}, u32[]{:S(2)}, u32[]{:S(2)}) collective-permute-start(f32[3,3,128]{2,1,0:T(4,128)S(1)} %get-tuple-element.1103), channel_id=1, source_target_pairs={{0,120},{8,0},{16,8},{24,16},{32,24},{40,32},{48,40},{56,48},{64,5... | collective-permute-start | bytes 13832 | tf_op jit(solution)/shard_map/ppermute | solution.py:15
  411.6 10.0 %collective-permute-start.52 = (f32[3,3,128]{2,1,0:T(4,128)S(1)}, f32[3,3,128]{2,1,0:T(4,128)S(1)}, u32[]{:S(2)}, u32[]{:S(2)}) collective-permute-start(f32[3,3,128]{2,1,0:T(4,128)S(1)} %collective-permute-done.51), channel_id=1, source_target_pairs={{1,0},{2,1},{3,2},{4,3},{5,4},{6,5},{7,6},{9,8},{10,9},{11,10},{12... | collective-permute-start | bytes 13832 | tf_op jit(solution)/shard_map/ppermute | solution.py:21
  413.5 10.1 %collective-permute-start.57 = (f32[3,3,128]{2,1,0:T(4,128)S(1)}, f32[3,3,128]{2,1,0:T(4,128)S(1)}, u32[]{:S(2)}, u32[]{:S(2)}) collective-permute-start(f32[3,3,128]{2,1,0:T(4,128)S(1)} %get-tuple-element.1110), channel_id=1, source_target_pairs={{0,120},{8,0},{16,8},{24,16},{32,24},{40,32},{48,40},{56,48},{64,5... | collective-permute-start | bytes 13832 | tf_op jit(solution)/shard_map/ppermute | solution.py:15
  416.0 7.6 %collective-permute-start.56 = (f32[3,3,128]{2,1,0:T(4,128)S(1)}, f32[3,3,128]{2,1,0:T(4,128)S(1)}, u32[]{:S(2)}, u32[]{:S(2)}) collective-permute-start(f32[3,3,128]{2,1,0:T(4,128)S(1)} %collective-permute-done.55), channel_id=1, source_target_pairs={{0,1},{1,2},{2,3},{3,4},{4,5},{5,6},{6,7},{8,9},{9,10},{10,11},{11... | collective-permute-start | bytes 13832 | tf_op jit(solution)/shard_map/ppermute | solution.py:21
  421.6 4.9 %collective-permute-start.59 = (f32[3,3,128]{2,1,0:T(4,128)S(1)}, f32[3,3,128]{2,1,0:T(4,128)S(1)}, u32[]{:S(2)}, u32[]{:S(2)}) collective-permute-start(f32[3,3,128]{2,1,0:T(4,128)S(1)} %collective-permute-done.58), channel_id=1, source_target_pairs={{1,0},{2,1},{3,2},{4,3},{5,4},{6,5},{7,6},{9,8},{10,9},{11,10},{12... | collective-permute-start | bytes 13832 | tf_op jit(solution)/shard_map/ppermute | solution.py:21
  (2 other events, 53.0 us)
